TPU v7x, 32 devices: a whole 2x2x4 slice. The times are simulated.
32 devices in a mesh: dp: 8 (over z, y), shard: 4 (over x, core).
Axes of the slice: x: 2, y: 2, z: 4, core: 2. Of those that a mesh axis runs over, the one named last changes fastest.
Arguments:
- tokens: bfloat16 [32768, 768], P(('dp', 'shard')), may hold values from -6 to 6
- teacher_tokens: bfloat16 [32768, 768], P(('dp', 'shard')), may hold values from -6 to 6
- cotangent: bfloat16 [32768, 768], P(('dp', 'shard')), may hold values from -6 to 6
- lengths: int32 [32], replicated, may hold values from 512 to 1024, as said below
- clip_scales: float32 [4], replicated, may hold values from 0.15 to 0.4
- attn_latent: float32 [4, 768, 768], P(None, ('dp', 'shard')), may hold values from -1 to 1
- up_latent: float32 [3072, 768], P(('dp', 'shard')), may hold values from -0.21875 to 0.21875
- down_latent: float32 [768, 3072], P(('dp', 'shard')), may hold values from -0.109375 to 0.109375
- biases: bfloat16 [5, 768], P(None, ('dp', 'shard')), may hold values from -1.1953125 to 1.1953125
- up_bias: bfloat16 [3072], P(('dp', 'shard')), may hold values from -1.1953125 to 1.1953125
- norm_gains: bfloat16 [2, 768], P(None, ('dp', 'shard')), may hold values from 0.5 to 1.5
- norm_shifts: bfloat16 [2, 768], P(None, ('dp', 'shard')), may hold values from -1.1953125 to 1.1953125
- teacher_attn: bfloat16 [4, 768, 768], P(None, ('dp', 'shard')), may hold values from -1 to 1
- teacher_up: bfloat16 [3072, 768], P(('dp', 'shard')), may hold values from -0.21875 to 0.21875
- teacher_down: bfloat16 [768, 3072], P(('dp', 'shard')), may hold values from -0.109375 to 0.109375
- teacher_biases: bfloat16 [5, 768], P(None, ('dp', 'shard')), may hold values from -1.1953125 to 1.1953125
- teacher_up_bias: bfloat16 [3072], P(('dp', 'shard')), may hold values from -1.1953125 to 1.1953125
- teacher_gains: bfloat16 [2, 768], P(None, ('dp', 'shard')), may hold values from 0.5 to 1.5
- teacher_shifts: bfloat16 [2, 768], P(None, ('dp', 'shard')), may hold values from -1.1953125 to 1.1953125
Outputs:
- output: bfloat16 [32768, 768], P(('dp', 'shard'))
- loss: float32 [], replicated
- input_grad: bfloat16 [32768, 768], P(('dp', 'shard'))
- attn_grad: float32 [4, 768, 768], P(None, ('dp', 'shard'))
- up_grad: float32 [3072, 768], P(('dp', 'shard'))
- down_grad: float32 [768, 3072], P(('dp', 'shard'))
- bias_grad: float32 [5, 768], P(None, ('dp', 'shard'))
- up_bias_grad: float32 [3072], P(('dp', 'shard'))
- gain_grad: float32 [2, 768], P(None, ('dp', 'shard'))
- shift_grad: float32 [2, 768], P(None, ('dp', 'shard'))
Inputs may be any that keep to these rules, and one draw needn't show every extreme that they name: The first lengths[s] positions of sequence s are tokens and the rest padding; some sequence has exactly 1024 and another exactly 512.
All inputs are finite; a program needn't handle non-finite values. Where the computation divides by a largest or mean magnitude, that divisor is 1e-20 or more.
Results may differ from a plain program's by a relative error of at most 0.012.
The roundings to bfloat16 on the way count: a program that leaves them out, or rounds other values in their place, can miss the bound.
Values may be sent and summed in bfloat16 or wider, within the bound.
A program may use at most 256 MiB of HBM per device.

v0:
```python
import math

import jax
import jax.numpy as jnp
from jax import lax
from jax.sharding import PartitionSpec as P

D = 768
HEADS = 12
HEAD_DIM = 64
SEQ_LEN = 1024


epsilon = 1e-05
masked_score = -1e30
hidden_weight = 0.25
saturation = 7.5


def project(inputs, weight):
    return lax.dot_general(
        inputs, weight, (((1,), (1,)), ((), ())), preferred_element_type=jnp.float32
    )


def outer_rows(left, right):
    return lax.dot_general(
        left, right, (((0,), (0,)), ((), ())), preferred_element_type=jnp.float32
    )


def binarize(latent):
    scale = jnp.mean(jnp.abs(latent), axis=-1, keepdims=True)
    return (scale * jnp.sign(latent)).astype(jnp.bfloat16)


def surrogate(latent):
    return jnp.mean(jnp.abs(latent), axis=-1, keepdims=True) * latent


def latent_grad(latent, grad):
    _, pull = jax.vjp(surrogate, latent)
    return pull(grad)[0]


def normalize(values):
    center = values - jnp.mean(values, axis=-1, keepdims=True)
    inverse = lax.rsqrt(jnp.mean(center * center, axis=-1, keepdims=True) + epsilon)
    return (center * inverse, inverse)


def norm_back(grad_norm, normed, inverse):
    return inverse * (
        grad_norm
        - jnp.mean(grad_norm, axis=-1, keepdims=True)
        - normed * jnp.mean(grad_norm * normed, axis=-1, keepdims=True)
    )


def clamp_act(values, scale):
    return saturation * scale * jnp.tanh(values / (saturation * scale))


def clamp_slope(values, scale):
    bent = jnp.tanh(values / (saturation * scale))
    return 1.0 - bent * bent


def live_softmax(scores, key_live):
    masked = jnp.where(key_live[None, None, :], scores, masked_score)
    top = jnp.max(masked, axis=-1, keepdims=True)
    expo = jnp.exp(masked - top)
    total = jnp.sum(expo, axis=-1, keepdims=True)
    return (expo / total, top[..., 0] + jnp.log(total[..., 0]))


def teacher_attend(query_seq, key_seq, value_seq, length):
    block_rows = min(512, SEQ_LEN)
    key_heads = key_seq.reshape(SEQ_LEN, HEADS, HEAD_DIM)
    value_heads = value_seq.reshape(SEQ_LEN, HEADS, HEAD_DIM)
    key_live = jnp.arange(SEQ_LEN, dtype=jnp.int32) < length

    def teacher_one_block(start):
        query_block = lax.dynamic_slice_in_dim(query_seq, start, block_rows, 0).reshape(
            block_rows, HEADS, HEAD_DIM
        )
        scores = jnp.einsum(
            "qhe,khe->hqk", query_block, key_heads, preferred_element_type=jnp.float32
        ) * HEAD_DIM ** (-0.5)
        probs, _ = live_softmax(scores, key_live)
        context = jnp.einsum(
            "hqk,khe->qhe",
            probs.astype(jnp.bfloat16),
            value_heads,
            preferred_element_type=jnp.float32,
        )
        return context.reshape(block_rows, D)

    starts = jnp.arange(SEQ_LEN // block_rows, dtype=jnp.int32) * block_rows
    return lax.map(teacher_one_block, starts).reshape(SEQ_LEN, D)


def student_attend(query_seq, key_seq, value_seq, tq_seq, tk_seq, length):
    block_rows = min(512, SEQ_LEN)
    key_heads = key_seq.reshape(SEQ_LEN, HEADS, HEAD_DIM)
    value_heads = value_seq.reshape(SEQ_LEN, HEADS, HEAD_DIM)
    teacher_keys = tk_seq.reshape(SEQ_LEN, HEADS, HEAD_DIM)
    key_live = jnp.arange(SEQ_LEN, dtype=jnp.int32) < length

    def student_one_block(start):
        query_block = lax.dynamic_slice_in_dim(query_seq, start, block_rows, 0).reshape(
            block_rows, HEADS, HEAD_DIM
        )
        teacher_block = lax.dynamic_slice_in_dim(tq_seq, start, block_rows, 0).reshape(
            block_rows, HEADS, HEAD_DIM
        )
        row_live = start + jnp.arange(block_rows, dtype=jnp.int32) < length
        scores = jnp.einsum(
            "qhe,khe->hqk", query_block, key_heads, preferred_element_type=jnp.float32
        ) * HEAD_DIM ** (-0.5)
        teacher_scores = jnp.einsum(
            "qhe,khe->hqk", teacher_block, teacher_keys, preferred_element_type=jnp.float32
        ) * HEAD_DIM ** (-0.5)
        pair_live = row_live[None, :, None] & key_live[None, None, :]
        differ = jnp.where(pair_live, scores - teacher_scores, 0.0)
        probs, logsum = live_softmax(scores, key_live)
        context = jnp.einsum(
            "hqk,khe->qhe",
            probs.astype(jnp.bfloat16),
            value_heads,
            preferred_element_type=jnp.float32,
        )
        return (context.reshape(block_rows, D), logsum, jnp.sum(differ * differ))

    starts = jnp.arange(SEQ_LEN // block_rows, dtype=jnp.int32) * block_rows
    contexts, logsums, squares = lax.map(student_one_block, starts)
    return (contexts.reshape(SEQ_LEN, D), logsums, jnp.sum(squares))


def attend_back(
    query_seq, key_seq, value_seq, tq_seq, tk_seq, dctx_seq, logsums, length, pair_norm
):
    block_rows = min(512, SEQ_LEN)
    key_heads = key_seq.reshape(SEQ_LEN, HEADS, HEAD_DIM)
    value_heads = value_seq.reshape(SEQ_LEN, HEADS, HEAD_DIM)
    teacher_keys = tk_seq.reshape(SEQ_LEN, HEADS, HEAD_DIM)
    key_live = jnp.arange(SEQ_LEN, dtype=jnp.int32) < length
    scaling = HEAD_DIM ** (-0.5)

    def attend_one_block(carry, items):
        key_acc, value_acc = carry
        start, logsum = items
        query_block = lax.dynamic_slice_in_dim(query_seq, start, block_rows, 0).reshape(
            block_rows, HEADS, HEAD_DIM
        )
        teacher_block = lax.dynamic_slice_in_dim(tq_seq, start, block_rows, 0).reshape(
            block_rows, HEADS, HEAD_DIM
        )
        grad_block = lax.dynamic_slice_in_dim(dctx_seq, start, block_rows, 0).reshape(
            block_rows, HEADS, HEAD_DIM
        )
        row_live = start + jnp.arange(block_rows, dtype=jnp.int32) < length
        scores = (
            jnp.einsum("qhe,khe->hqk", query_block, key_heads, preferred_element_type=jnp.float32)
            * scaling
        )
        teacher_scores = (
            jnp.einsum(
                "qhe,khe->hqk", teacher_block, teacher_keys, preferred_element_type=jnp.float32
            )
            * scaling
        )
        masked = jnp.where(key_live[None, None, :], scores, masked_score)
        probs = jnp.exp(masked - logsum[..., None])
        grad_probs = jnp.einsum(
            "qhe,khe->hqk", grad_block, value_heads, preferred_element_type=jnp.float32
        )
        weighted = jnp.sum(probs * grad_probs, axis=-1, keepdims=True)
        pair_live = row_live[None, :, None] & key_live[None, None, :]
        distill = jnp.where(pair_live, 2.0 * (scores - teacher_scores) / pair_norm, 0.0)
        grad_scores = (probs * (grad_probs - weighted) + distill).astype(jnp.bfloat16)
        grad_query = (
            jnp.einsum("hqk,khe->qhe", grad_scores, key_heads, preferred_element_type=jnp.float32)
            * scaling
        )
        key_acc = (
            key_acc
            + jnp.einsum(
                "hqk,qhe->khe", grad_scores, query_block, preferred_element_type=jnp.float32
            )
            * scaling
        )
        value_acc = value_acc + jnp.einsum(
            "hqk,qhe->khe",
            probs.astype(jnp.bfloat16),
            grad_block,
            preferred_element_type=jnp.float32,
        )
        return ((key_acc, value_acc), grad_query.reshape(block_rows, D))

    starts = jnp.arange(SEQ_LEN // block_rows, dtype=jnp.int32) * block_rows
    zeros = jnp.zeros((SEQ_LEN, HEADS, HEAD_DIM), jnp.float32)
    (key_acc, value_acc), grad_queries = lax.scan(
        attend_one_block, (zeros, zeros), (starts, logsums)
    )
    return (
        grad_queries.reshape(SEQ_LEN, D),
        key_acc.reshape(SEQ_LEN, D),
        value_acc.reshape(SEQ_LEN, D),
    )


def by_sequence(array):
    return array.reshape(array.shape[0] // SEQ_LEN, SEQ_LEN, array.shape[1])


def on_device(
    tokens,
    teacher_tokens,
    cotangent,
    lengths,
    clip_scales,
    attn_latent,
    up_latent,
    down_latent,
    biases,
    up_bias,
    norm_gains,
    norm_shifts,
    teacher_attn,
    teacher_up,
    teacher_down,
    teacher_biases,
    teacher_up_bias,
    teacher_gains,
    teacher_shifts,
):
    rows = tokens.shape[0]
    seq_count = rows // SEQ_LEN
    own_lengths = lax.dynamic_slice_in_dim(
        lengths, lax.axis_index(("dp", "shard")) * seq_count, seq_count
    )
    live_float = lengths.astype(jnp.float32)
    token_norm = jnp.sum(live_float)
    pair_norm = HEADS * jnp.sum(live_float * live_float)
    positions = jnp.arange(SEQ_LEN, dtype=jnp.int32)
    row_live = (positions[None, :] < own_lengths[:, None]).reshape(rows)
    student = (
        lax.all_gather(binarize(attn_latent), ("dp", "shard"), axis=1, tiled=True),
        lax.all_gather(binarize(up_latent), ("dp", "shard"), axis=0, tiled=True),
        lax.all_gather(binarize(down_latent), ("dp", "shard"), axis=0, tiled=True),
        lax.all_gather(biases, ("dp", "shard"), axis=1, tiled=True),
        lax.all_gather(up_bias, ("dp", "shard"), axis=0, tiled=True),
        lax.all_gather(norm_gains, ("dp", "shard"), axis=1, tiled=True),
        lax.all_gather(norm_shifts, ("dp", "shard"), axis=1, tiled=True),
    )
    attn_w, up_w, down_w, bias_w, up_b, gain_w, shift_w = student
    bias_float = bias_w.astype(jnp.float32)
    gain_float = gain_w.astype(jnp.float32)
    shift_float = shift_w.astype(jnp.float32)
    teacher = (
        lax.all_gather(teacher_attn, ("dp", "shard"), axis=1, tiled=True),
        lax.all_gather(teacher_up, ("dp", "shard"), axis=0, tiled=True),
        lax.all_gather(teacher_down, ("dp", "shard"), axis=0, tiled=True),
        lax.all_gather(teacher_biases, ("dp", "shard"), axis=1, tiled=True),
        lax.all_gather(teacher_up_bias, ("dp", "shard"), axis=0, tiled=True),
        lax.all_gather(teacher_gains, ("dp", "shard"), axis=1, tiled=True),
        lax.all_gather(teacher_shifts, ("dp", "shard"), axis=1, tiled=True),
    )
    teach_attn, teach_up, teach_down, teach_bias, teach_up_bias, teach_gain, teach_shift = teacher
    teach_bias_float = teach_bias.astype(jnp.float32)
    teach_qkv = (
        project(teacher_tokens, teach_attn[:3].reshape(3 * D, D))
        + teach_bias_float[:3].reshape(3 * D)
    ).astype(jnp.bfloat16)
    teach_query, teach_key, teach_value = (
        teach_qkv[:, :D],
        teach_qkv[:, D : 2 * D],
        teach_qkv[:, 2 * D :],
    )
    teach_context = (
        lax.map(
            lambda items: teacher_attend(*items),
            (
                by_sequence(teach_query),
                by_sequence(teach_key),
                by_sequence(teach_value),
                own_lengths,
            ),
        )
        .reshape(rows, D)
        .astype(jnp.bfloat16)
    )
    teach_normed, _ = normalize(
        teacher_tokens.astype(jnp.float32)
        + project(teach_context, teach_attn[3])
        + teach_bias_float[3]
    )
    teach_hidden = teach_normed * teach_gain[0].astype(jnp.float32) + teach_shift[0].astype(
        jnp.float32
    )
    teach_upper = project(teach_hidden.astype(jnp.bfloat16), teach_up) + teach_up_bias.astype(
        jnp.float32
    )
    teach_lower = (
        project(jax.nn.gelu(teach_upper, approximate=False).astype(jnp.bfloat16), teach_down)
        + teach_bias_float[4]
    )
    teach_final, _ = normalize(teach_hidden + teach_lower)
    teach_out = teach_final * teach_gain[1].astype(jnp.float32) + teach_shift[1].astype(jnp.float32)
    x_float = tokens.astype(jnp.float32)
    x_low = clamp_act(x_float, clip_scales[0]).astype(jnp.bfloat16)
    qkv_low = (project(x_low, attn_w[:3].reshape(3 * D, D)) + bias_float[:3].reshape(3 * D)).astype(
        jnp.bfloat16
    )
    queries, keys_all, values_all = (qkv_low[:, :D], qkv_low[:, D : 2 * D], qkv_low[:, 2 * D :])
    contexts, logsums, squares = lax.map(
        lambda items: student_attend(*items),
        (
            by_sequence(queries),
            by_sequence(keys_all),
            by_sequence(values_all),
            by_sequence(teach_query),
            by_sequence(teach_key),
            own_lengths,
        ),
    )
    context = contexts.reshape(rows, D)
    ctx_low = clamp_act(context, clip_scales[1]).astype(jnp.bfloat16)
    first_normed, first_inverse = normalize(x_float + project(ctx_low, attn_w[3]) + bias_float[3])
    hidden = first_normed * gain_float[0] + shift_float[0]
    hidden_low = clamp_act(hidden, clip_scales[2]).astype(jnp.bfloat16)
    upper = project(hidden_low, up_w) + up_b.astype(jnp.float32)
    gelu_out = jax.nn.gelu(upper, approximate=False)
    gelu_low = clamp_act(gelu_out, clip_scales[3]).astype(jnp.bfloat16)
    lower = project(gelu_low, down_w) + bias_float[4]
    second_normed, second_inverse = normalize(hidden + lower)
    result = second_normed * gain_float[1] + shift_float[1]
    gap = jnp.where(row_live[:, None], result - teach_out, 0.0)
    local_loss = jnp.sum(gap * gap) / (D * token_norm) + jnp.sum(squares) / pair_norm
    loss = lax.psum(local_loss, ("dp", "shard"))
    back_attn, back_up, back_down = (
        lax.all_gather(binarize(attn_latent), ("dp", "shard"), axis=1, tiled=True),
        lax.all_gather(binarize(up_latent), ("dp", "shard"), axis=0, tiled=True),
        lax.all_gather(binarize(down_latent), ("dp", "shard"), axis=0, tiled=True),
    )
    grad_out = cotangent.astype(jnp.float32) + gap * (2.0 * hidden_weight)
    gain_two = jnp.sum(grad_out * second_normed, axis=0)
    shift_two = jnp.sum(grad_out, axis=0)
    grad_second = norm_back(grad_out * gain_float[1], second_normed, second_inverse)
    grad_lower = grad_second.astype(jnp.bfloat16)
    down_bias_grad = jnp.sum(grad_lower.astype(jnp.float32), axis=0)
    down_weight_grad = outer_rows(grad_lower, gelu_low)
    grad_gelu = jnp.dot(grad_lower, back_down, preferred_element_type=jnp.float32) * clamp_slope(
        gelu_out, clip_scales[3]
    )
    slope = 0.5 * (1.0 + lax.erf(upper * (1.0 / math.sqrt(2.0)))) + upper * jnp.exp(
        -0.5 * upper * upper
    ) * (1.0 / math.sqrt(2.0 * math.pi))
    grad_upper = (grad_gelu * slope).astype(jnp.bfloat16)
    up_bias_grad = jnp.sum(grad_upper.astype(jnp.float32), axis=0)
    up_weight_grad = outer_rows(grad_upper, hidden_low)
    grad_hidden = grad_second + jnp.dot(
        grad_upper, back_up, preferred_element_type=jnp.float32
    ) * clamp_slope(hidden, clip_scales[2])
    gain_one = jnp.sum(grad_hidden * first_normed, axis=0)
    shift_one = jnp.sum(grad_hidden, axis=0)
    grad_first = norm_back(grad_hidden * gain_float[0], first_normed, first_inverse)
    grad_attn_out = grad_first.astype(jnp.bfloat16)
    out_bias_grad = jnp.sum(grad_attn_out.astype(jnp.float32), axis=0)
    out_weight_grad = outer_rows(grad_attn_out, ctx_low)
    grad_context = (
        jnp.dot(grad_attn_out, back_attn[3], preferred_element_type=jnp.float32)
        * clamp_slope(context, clip_scales[1])
    ).astype(jnp.bfloat16)
    grad_queries, grad_keys, grad_values = lax.map(
        lambda items: attend_back(*items, pair_norm),
        (
            by_sequence(queries),
            by_sequence(keys_all),
            by_sequence(values_all),
            by_sequence(teach_query),
            by_sequence(teach_key),
            by_sequence(grad_context),
            logsums,
            own_lengths,
        ),
    )
    grad_qkv = jnp.concatenate(
        [grad_queries.reshape(rows, D), grad_keys.reshape(rows, D), grad_values.reshape(rows, D)],
        axis=1,
    ).astype(jnp.bfloat16)
    qkv_bias_grad = jnp.sum(grad_qkv.astype(jnp.float32), axis=0).reshape(3, D)
    qkv_weight_grad = outer_rows(grad_qkv, x_low).reshape(3, D, D)
    grad_input = jnp.dot(
        grad_qkv, back_attn[:3].reshape(3 * D, D), preferred_element_type=jnp.float32
    )
    input_grad = (grad_first + grad_input * clamp_slope(x_float, clip_scales[0])).astype(
        jnp.bfloat16
    )
    attn_weight_grad = jnp.concatenate([qkv_weight_grad, out_weight_grad[None]], axis=0)
    bias_terms = jnp.concatenate([qkv_bias_grad, out_bias_grad[None], down_bias_grad[None]], axis=0)
    gain_terms = jnp.stack([gain_one, gain_two])
    shift_terms = jnp.stack([shift_one, shift_two])
    summed = (
        lax.psum_scatter(attn_weight_grad, ("dp", "shard"), scatter_dimension=1, tiled=True),
        lax.psum_scatter(up_weight_grad, ("dp", "shard"), scatter_dimension=0, tiled=True),
        lax.psum_scatter(down_weight_grad, ("dp", "shard"), scatter_dimension=0, tiled=True),
        lax.psum_scatter(bias_terms, ("dp", "shard"), scatter_dimension=1, tiled=True),
        lax.psum_scatter(up_bias_grad, ("dp", "shard"), scatter_dimension=0, tiled=True),
        lax.psum_scatter(gain_terms, ("dp", "shard"), scatter_dimension=1, tiled=True),
        lax.psum_scatter(shift_terms, ("dp", "shard"), scatter_dimension=1, tiled=True),
    )
    attn_total, up_total, down_total, bias_total, up_bias_total, gain_total, shift_total = summed
    return (
        result.astype(jnp.bfloat16),
        loss,
        input_grad,
        latent_grad(attn_latent, attn_total),
        latent_grad(up_latent, up_total),
        latent_grad(down_latent, down_total),
        bias_total,
        up_bias_total,
        gain_total,
        shift_total,
    )


def solution(mesh):
    in_specs = (
        P(("dp", "shard"), None),
        P(("dp", "shard"), None),
        P(("dp", "shard"), None),
        P(),
        P(),
        P(None, ("dp", "shard"), None),
        P(("dp", "shard"), None),
        P(("dp", "shard"), None),
        P(None, ("dp", "shard")),
        P(("dp", "shard")),
        P(None, ("dp", "shard")),
        P(None, ("dp", "shard")),
        P(None, ("dp", "shard"), None),
        P(("dp", "shard"), None),
        P(("dp", "shard"), None),
        P(None, ("dp", "shard")),
        P(("dp", "shard")),
        P(None, ("dp", "shard")),
        P(None, ("dp", "shard")),
    )
    out_specs = (
        P(("dp", "shard"), None),
        P(),
        P(("dp", "shard"), None),
        P(None, ("dp", "shard"), None),
        P(("dp", "shard"), None),
        P(("dp", "shard"), None),
        P(None, ("dp", "shard")),
        P(("dp", "shard")),
        P(None, ("dp", "shard")),
        P(None, ("dp", "shard")),
    )
    return jax.shard_map(
        on_device, mesh=mesh, in_specs=in_specs, out_specs=out_specs, check_vma=False
    )
```

profile of v0, /device:TPU:0, one launch (start us, length us, event | category | flops | bytes accessed | tf_op | source)
XLA Modules:
  0.0 1094.0 jit_solution(9773358400201907683)
XLA Ops:
  19.5 44.0 %all-gather.1 = bf16[32,24,5]{1,2,0:T(8,128)(2,1)S(1)} all-gather(bf16[1,24,5]{1,2,0:T(8,128)(2,1)} %bitcast.299), channel_id=1, replica_groups=mesh['dp'=8,'shard'=4] {'dp','shard'}, dimensions={0}, use_global_device_ids=true | all-gather | bytes 7920 | tf_op jit(solution)/shard_map/all_gather | solution.py:265
  64.4 37.0 %all-gather = bf16[32,24,5]{1,2,0:T(8,128)(2,1)S(1)} all-gather(bf16[1,24,5]{1,2,0:T(8,128)(2,1)S(1)} %bitcast.300), channel_id=1, replica_groups=mesh['dp'=8,'shard'=4] {'dp','shard'}, dimensions={0}, use_global_device_ids=true | all-gather | bytes 7920 | tf_op jit(solution)/shard_map/all_gather | solution.py:252
  106.7 37.8 %all-reduce.7 = (bf16[3072]{0:T(1024)(128)(2,1)S(1)}, bf16[3072]{0:T(1024)(128)(2,1)S(1)}) all-reduce(bf16[3072]{0:T(1024)(128)(2,1)S(1)} %dynamic-update-slice, bf16[3072]{0:T(1024)(128)(2,1)S(1)} %dynamic-update-slice.1), channel_id=1, replica_groups=mesh['dp'=8,'shard'=4] {'dp','shard'}, use_global_device_ids=true, to_apply=%add | all-reduce | flops 6144 | bytes 24576
  145.1 40.6 %all-gather.4 = bf16[32,24,2]{1,2,0:T(2,128)(2,1)S(1)} all-gather(bf16[1,24,2]{1,2,0:T(2,128)(2,1)S(1)} %bitcast.301), channel_id=1, replica_groups=mesh['dp'=8,'shard'=4] {'dp','shard'}, dimensions={0}, use_global_device_ids=true | all-gather | bytes 3168 | tf_op jit(solution)/shard_map/all_gather | solution.py:267
  185.8 36.5 %all-gather.5 = bf16[32,24,2]{1,2,0:T(2,128)(2,1)S(1)} all-gather(bf16[1,24,2]{1,2,0:T(2,128)(2,1)S(1)} %bitcast.302), channel_id=1, replica_groups=mesh['dp'=8,'shard'=4] {'dp','shard'}, dimensions={0}, use_global_device_ids=true | all-gather | bytes 3168 | tf_op jit(solution)/shard_map/all_gather | solution.py:268
  227.2 37.8 %all-gather.2 = bf16[32,24,2]{1,2,0:T(2,128)(2,1)S(1)} all-gather(bf16[1,24,2]{1,2,0:T(2,128)(2,1)S(1)} %bitcast.303), channel_id=1, replica_groups=mesh['dp'=8,'shard'=4] {'dp','shard'}, dimensions={0}, use_global_device_ids=true | all-gather | bytes 3168 | tf_op jit(solution)/shard_map/all_gather | solution.py:254
  265.3 36.7 %all-gather.3 = bf16[32,24,2]{1,2,0:T(2,128)(2,1)S(1)} all-gather(bf16[1,24,2]{1,2,0:T(2,128)(2,1)S(1)} %bitcast.304), channel_id=1, replica_groups=mesh['dp'=8,'shard'=4] {'dp','shard'}, dimensions={0}, use_global_device_ids=true | all-gather | bytes 3168 | tf_op jit(solution)/shard_map/all_gather | solution.py:255
  322.5 67.6 %while.76 = (s32[]{:T(128)}, bf16[2,512,768]{2,1,0:T(8,128)(2,1)}, s32[2]{0:T(128)S(1)}, bf16[1024,768]{0,1:T(8,128)(2,1)S(1)}, bf16[1024,12,64]{0,2,1:T(8,128)(...) while((s32[]{:T(128)}, bf16[2,512,768]{2,1,0:T(8,128)(2,1)}, s32[2]{0:T(128)S(1)}, ...), condition=%wide.region_15.16_spmd.clone.clone, body=%wide.region_12.15_spmd.clone.sunk.clone | while | flops 1648363520 | bytes 59820672 | solution.py:100
  327.0 13.5 %fusion.255 = (f32[12,512]{1,0:T(8,128)S(1)}, f32[12,512,1024]{2,1,0:T(8,128)}) fusion(pred[1024]{0:T(1024)(128)(4,1)S(1)} %iota_compare_fusion.10, bf16[512,12,64]{0,2,1:T(8,128)(2,1)} %bitcast.273, bf16[1024,12,64]{0,2,1:T(8,128)(2,1)S(1)} %get-tuple-element.1166), kind=kOutput, calls=%fused_computation.261.clone.1.clone | convolution fusion | flops 830473216 | bytes 27550720 | tf_op jit(solution)/shard_map/while/body/eval_jaxpr/while/body/eval_jaxpr/sub | solution.py:72
  340.4 11.6 %fusion.256 = bf16[12,512,64]{1,2,0:T(8,128)(2,1)} fusion(bf16[1024,12,64]{0,2,1:T(8,128)(2,1)} %get-tuple-element.1167, f32[12,512,1024]{2,1,0:T(8,128)} %get-tuple-element.1039, f32[12,512]{1,0:T(8,128)S(1)} %get-tuple-element.1040), kind=kOutput, calls=%fused_computation.11.clone.1.clone | convolution fusion | flops 817889280 | bytes 27549696 | tf_op jit(solution)/shard_map/while/body/eval_jaxpr/while/body/eval_jaxpr/hqk,khe->qhe/dot_general | solution.py:91
  360.8 13.3 %fusion.255 = (f32[12,512]{1,0:T(8,128)S(1)}, f32[12,512,1024]{2,1,0:T(8,128)}) fusion(pred[1024]{0:T(1024)(128)(4,1)S(1)} %iota_compare_fusion.10, bf16[512,12,64]{0,2,1:T(8,128)(2,1)} %bitcast.273, bf16[1024,12,64]{0,2,1:T(8,128)(2,1)S(1)} %get-tuple-element.1166), kind=kOutput, calls=%fused_computation.261.clone.1.clone | convolution fusion | flops 830473216 | bytes 27550720 | tf_op jit(solution)/shard_map/while/body/eval_jaxpr/while/body/eval_jaxpr/sub | solution.py:72
  374.1 11.6 %fusion.256 = bf16[12,512,64]{1,2,0:T(8,128)(2,1)} fusion(bf16[1024,12,64]{0,2,1:T(8,128)(2,1)} %get-tuple-element.1167, f32[12,512,1024]{2,1,0:T(8,128)} %get-tuple-element.1039, f32[12,512]{1,0:T(8,128)S(1)} %get-tuple-element.1040), kind=kOutput, calls=%fused_computation.11.clone.1.clone | convolution fusion | flops 817889280 | bytes 27549696 | tf_op jit(solution)/shard_map/while/body/eval_jaxpr/while/body/eval_jaxpr/hqk,khe->qhe/dot_general | solution.py:91
  397.1 37.0 %fusion.78.clone.4 = bf16[1024,3072]{1,0:T(8,128)(2,1)} fusion(f32[3072]{0:T(1024)S(1)} %copy-done.52, bf16[3072,768]{1,0:T(8,128)(2,1)} %all-gather.21.cloned.1.call-done, f32[1024,768]{0,1:T(8,128)} %copy-done.24, f32[768]{0:T(1024)S(1)} %copy-done.60, f32[768]{0:T(1024)S(1)} %copy-done.61, ...), kind=kOutput, calls=%fused_computation.71.clone.clone.clone.clone.clone.clone.1 | convolution fusion | flops 5043388416 | bytes 14182400 | tf_op jit(solution)/shard_map/dot_general | solution.py:21
  461.5 125.1 %while.77 = (s32[]{:T(128)}, f32[2,512,768]{2,1,0:T(8,128)}, f32[2,12,512]{2,1,0:T(8,128)}, f32[2]{0:T(128)S(1)}, s32[2]{0:T(128)S(1)}, /*index=5*/bf16[1024,768...) while((s32[]{:T(128)}, f32[2,512,768]{2,1,0:T(8,128)}, ...), condition=%wide.region_5.6_spmd.clone.clone.clone, body=%wide.region_1.5_spmd.clone.clone.sunk.clone | while | flops 2529685504 | bytes 125517024 | solution.py:136
  477.9 11.3 %fusion.262 = f32[12,512]{1,0:T(8,128)S(1)} fusion(f32[12,512,1024]{2,1,0:T(8,128)} %get-tuple-element.1064, f32[12,512]{1,0:T(8,128)S(1)} %get-tuple-element.1065, pred[1024]{0:T(1024)(128)(4,1)S(1)} %iota_compare_fusion.11), kind=kLoop, calls=%fused_computation.22.clone.1.clone | loop fusion | flops 25159680 | bytes 25216000 | tf_op jit(solution)/shard_map/while/body/eval_jaxpr/while/body/eval_jaxpr/reduce_sum | solution.py:73
  489.9 12.3 %fusion.263 = f32[12,512,64]{1,2,0:T(8,128)} fusion(bf16[1024,12,64]{0,2,1:T(8,128)(2,1)S(1)} %copy-done.33, f32[12,512,1024]{2,1,0:T(8,128)} %get-tuple-element.1064, f32[12,512]{1,0:T(8,128)S(1)} %fusion.262, f32[12,512]{1,0:T(8,128)S(1)} %get-tuple-element.1065, pred[1024]{0:T(1024)(128)(4,1)S(1)} %iota_compare_fusion.11), kind=kOutput, calls=%fused_computation.23.clone.1.clone | convolution fusion | flops 836763648 | bytes 28361728 | tf_op jit(solution)/shard_map/while/body/eval_jaxpr/while/body/eval_jaxpr/hqk,khe->qhe/dot_general | solution.py:127
  509.6 13.8 %multiply_reduce_fusion.19 = f32[]{:T(128)} fusion(f32[12,512,1024]{2,1,0:T(8,128)} %get-tuple-element.1064, pred[512,1024]{1,0:T(8,128)(4,1)S(1)} %broadcast_and_fusion.6, bf16[512,12,64]{0,2,1:T(8,128)(2,1)} %bitcast.276, bf16[1024,12,64]{0,2,1:T(8,128)(2,1)S(1)} %get-tuple-element.1147), kind=kOutput, calls=%fused_computation.18.clone.1.clone | convolution fusion | flops 843055104 | bytes 28049412 | tf_op jit(solution)/shard_map/while/body/eval_jaxpr/while/body/eval_jaxpr/qhe,khe->hqk/dot_general | solution.py:121
  540.4 11.3 %fusion.262 = f32[12,512]{1,0:T(8,128)S(1)} fusion(f32[12,512,1024]{2,1,0:T(8,128)} %get-tuple-element.1064, f32[12,512]{1,0:T(8,128)S(1)} %get-tuple-element.1065, pred[1024]{0:T(1024)(128)(4,1)S(1)} %iota_compare_fusion.11), kind=kLoop, calls=%fused_computation.22.clone.1.clone | loop fusion | flops 25159680 | bytes 25216000 | tf_op jit(solution)/shard_map/while/body/eval_jaxpr/while/body/eval_jaxpr/reduce_sum | solution.py:73
  552.4 12.3 %fusion.263 = f32[12,512,64]{1,2,0:T(8,128)} fusion(bf16[1024,12,64]{0,2,1:T(8,128)(2,1)S(1)} %copy-done.33, f32[12,512,1024]{2,1,0:T(8,128)} %get-tuple-element.1064, f32[12,512]{1,0:T(8,128)S(1)} %fusion.262, f32[12,512]{1,0:T(8,128)S(1)} %get-tuple-element.1065, pred[1024]{0:T(1024)(128)(4,1)S(1)} %iota_compare_fusion.11), kind=kOutput, calls=%fused_computation.23.clone.1.clone | convolution fusion | flops 836763648 | bytes 28361728 | tf_op jit(solution)/shard_map/while/body/eval_jaxpr/while/body/eval_jaxpr/hqk,khe->qhe/dot_general | solution.py:127
  572.0 13.8 %multiply_reduce_fusion.19 = f32[]{:T(128)} fusion(f32[12,512,1024]{2,1,0:T(8,128)} %get-tuple-element.1064, pred[512,1024]{1,0:T(8,128)(4,1)S(1)} %broadcast_and_fusion.6, bf16[512,12,64]{0,2,1:T(8,128)(2,1)} %bitcast.276, bf16[1024,12,64]{0,2,1:T(8,128)(2,1)S(1)} %get-tuple-element.1147), kind=kOutput, calls=%fused_computation.18.clone.1.clone | convolution fusion | flops 843055104 | bytes 28049412 | tf_op jit(solution)/shard_map/while/body/eval_jaxpr/while/body/eval_jaxpr/qhe,khe->hqk/dot_general | solution.py:121
  596.9 40.3 %fusion.44 = (f32[1024,3072]{1,0:T(8,128)}, f32[1024,3072]{1,0:T(8,128)}) fusion(f32[3072]{0:T(1024)S(1)} %copy-done.50, f32[]{:T(128)} %bitcast.22, bf16[3072,768]{1,0:T(8,128)(2,1)} %all-gather.17.cloned.1.call-done, f32[]{:T(128)} %bitcast.23, f32[768]{0:T(1024)S(1)} %copy-done.57, f32[768]{0:T(1024)S(1)} %copy-done.47, f32[1024]{0:T(1024)S(1)} %add_rsqrt_fusion.3, ...), kind=kOutput, calls=%fused_computation.68 | convolution fusion | flops 5044961280 | bytes 33056776 | tf_op jit(solution)/shard_map/dot_general | solution.py:21
  667.0 20.4 %convert_reduce_fusion = (f32[3072]{0:T(1024)}, bf16[1024,3072]{1,0:T(8,128)(2,1)S(1)}) fusion(f32[1024,3072]{1,0:T(8,128)} %get-tuple-element.806, f32[3072]{0:T(1024)S(1)} %copy-done.50, f32[1024,3072]{1,0:T(8,128)} %get-tuple-element.805, bf16[768,3072]{1,0:T(8,128)(2,1)} %all-gather.19.cloned.1.call-done, f32[1024,768]{0,1:T(8,128)} %copy-done.26), kind=kOutput, calls=%fused_computation.78 | convolution fusion | flops 4882953216 | bytes 39346176 | tf_op jit(solution)/shard_map/dot_general | solution.py:354
  715.5 210.6 %while.78 = (s32[]{:T(128)}, f32[1024,12,64]{0,2,1:T(8,128)}, f32[1024,12,64]{0,2,1:T(8,128)}, bf16[2,512,768]{2,1,0:T(8,128)(2,1)}, s32[2]{0:T(128)S(1)}, /*ind...) while((s32[]{:T(128)}, f32[1024,12,64]{0,2,1:T(8,128)}, ...), condition=%wide.region_31.32_spmd.clone.clone.clone.clone, body=%wide.region_29.31_spmd.clone.clone.clone.sunk.clone | while | flops 5768225792 | bytes 213489472 | solution.py:203
  730.8 10.4 fusion.280
  744.8 40.1 %add_convert_fusion.6 = bf16[12,512,1024]{2,1,0:T(8,128)(2,1)} fusion(f32[12,512,1024]{2,1,0:T(8,128)} %fusion.280, f32[12,512,1024]{2,1,0:T(8,128)} %fusion.281, f32[]{:T(128)} %get-tuple-element.1210, f32[12,512]{1,0:T(8,128)S(1)} %dynamic-slice_bitcast_fusion.3, pred[512,1024]{1,0:T(8,128)(4,1)S(1)} %broadcast_and_fusion.7, ...), kind=kOutput, calls=%fused_computation.34.clone.1.clone | convolution fusion | flops 1711283200 | bytes 65823748 | tf_op jit(solution)/shard_map/while/body/eval_jaxpr/while/body/eval_jaxpr/sub | solution.py:181
  805.5 13.6 %bitcast_add_fusion.7 = f32[1024,12,64]{0,2,1:T(8,128)} fusion(f32[1024,12,64]{0,2,1:T(8,128)} %get-tuple-element.1185, bf16[512,12,64]{0,2,1:T(8,128)(2,1)S(1)} %bitcast.272, f32[12,512,1024]{2,1,0:T(8,128)} %fusion.281, f32[12,512]{1,0:T(8,128)S(1)} %dynamic-slice_bitcast_fusion.3, pred[1024]{0:T(1024)(128)(4,1)S(1)} %iota_compare_fusion.12, ...), kind=kOutput, calls=%fused_computation.46.clone.1.clone | convolution fusion | flops 832045056 | bytes 32269312 | tf_op jit(solution)/shard_map/while/body/eval_jaxpr/while/body/eval_jaxpr/hqk,qhe->khe/dot_general | solution.py:193
  823.8 11.1 %fusion.281 = f32[12,512,1024]{2,1,0:T(8,128)} fusion(bf16[512,12,64]{0,2,1:T(8,128)(2,1)S(1)} %bitcast.265, bf16[1024,12,64]{0,2,1:T(8,128)(2,1)S(1)} %get-tuple-element.1203), kind=kOutput, calls=%fused_computation.270.clone.1.clone | convolution fusion | flops 805306368 | bytes 27525120 | tf_op jit(solution)/shard_map/while/body/eval_jaxpr/while/body/eval_jaxpr/qhe,khe->hqk/dot_general | solution.py:164
  834.8 11.0 %fusion.280 = f32[12,512,1024]{2,1,0:T(8,128)} fusion(bf16[512,12,64]{0,2,1:T(8,128)(2,1)S(1)} %bitcast.268, bf16[1024,12,64]{0,2,1:T(8,128)(2,1)S(1)} %copy-done.4), kind=kOutput, calls=%fused_computation.271.clone.1.clone | convolution fusion | flops 805306368 | bytes 27525120 | tf_op jit(solution)/shard_map/while/body/eval_jaxpr/while/body/eval_jaxpr/qhe,khe->hqk/dot_general | solution.py:168
  849.5 40.1 %add_convert_fusion.6 = bf16[12,512,1024]{2,1,0:T(8,128)(2,1)} fusion(f32[12,512,1024]{2,1,0:T(8,128)} %fusion.280, f32[12,512,1024]{2,1,0:T(8,128)} %fusion.281, f32[]{:T(128)} %get-tuple-element.1210, f32[12,512]{1,0:T(8,128)S(1)} %dynamic-slice_bitcast_fusion.3, pred[512,1024]{1,0:T(8,128)(4,1)S(1)} %broadcast_and_fusion.7, ...), kind=kOutput, calls=%fused_computation.34.clone.1.clone | convolution fusion | flops 1711283200 | bytes 65823748 | tf_op jit(solution)/shard_map/while/body/eval_jaxpr/while/body/eval_jaxpr/sub | solution.py:181
  911.8 14.2 %bitcast_add_fusion.7 = f32[1024,12,64]{0,2,1:T(8,128)} fusion(f32[1024,12,64]{0,2,1:T(8,128)} %get-tuple-element.1185, bf16[512,12,64]{0,2,1:T(8,128)(2,1)S(1)} %bitcast.272, f32[12,512,1024]{2,1,0:T(8,128)} %fusion.281, f32[12,512]{1,0:T(8,128)S(1)} %dynamic-slice_bitcast_fusion.3, pred[1024]{0:T(1024)(128)(4,1)S(1)} %iota_compare_fusion.12, ...), kind=kOutput, calls=%fused_computation.46.clone.1.clone | convolution fusion | flops 832045056 | bytes 32269312 | tf_op jit(solution)/shard_map/while/body/eval_jaxpr/while/body/eval_jaxpr/hqk,qhe->khe/dot_general | solution.py:193
  950.5 38.1 %all-reduce.6 = (f32[]{:T(128)}, f32[5,768]{1,0:T(8,128)S(1)}, f32[3072]{0:T(1024)S(1)}, f32[2,768]{1,0:T(2,128)S(1)}, f32[2,768]{1,0:T(2,128)S(1)}) all-reduce(f32[]{:T(128)S(6)} %add.321, f32[5,768]{1,0:T(8,128)S(1)} %pad_maximum_fusion.2, f32[3072]{0:T(1024)S(1)} %copy-done.53, ...), channel_id=1, replica_groups=mesh['dp'=8,'shard'=4] {'dp','shard'}, use_global_device_ids=true, to_apply=%region_24.25 | all-reduce | flops 9985 | bytes 79880 | tf_op jit(solution)/shard_map/psum | solution.py:341
  1006.3 74.4 %reduce-scatter.7.cloned.1.call-done = f32[4,24,768]{2,1,0:T(8,128)} async-done(((f32[4,768,768]{2,1,0:T(8,128)}), f32[4,24,768]{2,1,0:T(8,128)}) %reduce-scatter.7.cloned.1.call-update) | async-done | bytes 294928 | tf_op jit(solution)/shard_map/reduce_scatter | solution.py:406
  (392 shorter events, 315.1 us)
Async XLA Ops:
  7.2 57.3 %copy-start.64 = (bf16[5,24]{1,0:T(8,128)(2,1)S(1)}, bf16[5,24]{1,0:T(8,128)(2,1)}, u32[]{:S(2)}) copy-start(bf16[5,24]{1,0:T(8,128)(2,1)} %param.33) | copy-start | bytes 724
  7.2 302.1 %all-gather.15.cloned.1.call-start = ((), (), s32[]{:S(2)}) async-start(), calls=%async_computation.4 | async-start | bytes 4866048 | tf_op jit(solution)/shard_map/all_gather | solution.py:262
  7.9 389.1 %all-gather.21.cloned.1.call-start = ((), (), s32[]{:S(2)}) async-start(), calls=%async_computation.7 | async-start | bytes 4866048 | tf_op jit(solution)/shard_map/all_gather | solution.py:263
  8.7 425.5 %all-gather.23.cloned.1.call-start = ((), (), s32[]{:S(2)}) async-start(), calls=%async_computation.8 | async-start | bytes 4866048 | tf_op jit(solution)/shard_map/all_gather | solution.py:264
  9.4 436.3 %all-gather.13.cloned.1.call-start = ((), (), s32[]{:S(2)}) async-start(), calls=%async_computation.3 | async-start | bytes 4866048 | tf_op jit(solution)/shard_map/all_gather | solution.py:249
  12.8 584.0 %all-gather.17.cloned.1.call-start = ((), (), s32[]{:S(2)}) async-start(), calls=%async_computation.5 | async-start | bytes 4866048 | tf_op jit(solution)/shard_map/all_gather | solution.py:250
  16.2 621.0 %all-gather.19.cloned.1.call-start = ((), (), s32[]{:S(2)}) async-start(), calls=%async_computation.6 | async-start | bytes 4866048 | tf_op jit(solution)/shard_map/all_gather | solution.py:251
  17.4 88.8 %copy-start.74 = (bf16[96]{0:T(256)(128)(2,1)S(1)}, bf16[96]{0:T(256)(128)(2,1)}, u32[]{:S(2)}) copy-start(bf16[96]{0:T(256)(128)(2,1)} %param.34) | copy-start | bytes 580
  17.4 89.0 %copy-start.75 = (bf16[96]{0:T(256)(128)(2,1)S(1)}, bf16[96]{0:T(256)(128)(2,1)}, u32[]{:S(2)}) copy-start(bf16[96]{0:T(256)(128)(2,1)} %param.41) | copy-start | bytes 580
  17.4 127.7 %copy-start.70 = (bf16[2,24]{1,0:T(2,128)(2,1)S(1)}, bf16[2,24]{1,0:T(2,128)(2,1)}, u32[]{:S(2)}) copy-start(bf16[2,24]{1,0:T(2,128)(2,1)} %param.42) | copy-start | bytes 292
  17.4 168.4 %copy-start.71 = (bf16[2,24]{1,0:T(2,128)(2,1)S(1)}, bf16[2,24]{1,0:T(2,128)(2,1)}, u32[]{:S(2)}) copy-start(bf16[2,24]{1,0:T(2,128)(2,1)} %param.43) | copy-start | bytes 292
  17.4 205.0 %copy-start.54 = (f32[4]{0:T(128)S(1)}, f32[4]{0:T(128)}, u32[]{:S(2)}) copy-start(f32[4]{0:T(128)} %param.29) | copy-start | bytes 52
  17.5 205.6 %copy-start.28 = (bf16[1024,768]{1,0:T(8,128)(2,1)S(1)}, bf16[1024,768]{1,0:T(8,128)(2,1)}, u32[]{:S(2)}) copy-start(bf16[1024,768]{1,0:T(8,128)(2,1)} %param.25) | copy-start | bytes 4718596
  19.3 984.7 %reduce-scatter.11.cloned.1.call-start = ((), (), s32[]{:S(2)}) async-start(), calls=%async_computation.11 | async-start | bytes 9732096 | tf_op jit(solution)/shard_map/reduce_scatter | solution.py:408
  19.5 205.2 %copy-start.9 = (bf16[2,512,768]{2,1,0:T(8,128)(2,1)}, bf16[2,512,768]{2,1,0:T(8,128)(2,1)S(1)}, u32[]{:S(2)}) copy-start(bf16[2,512,768]{2,1,0:T(8,128)(2,1)S(1)} %fusion.130) | copy-start | bytes 4718596
  102.4 124.8 %copy-start.72 = (bf16[2,24]{1,0:T(2,128)(2,1)S(1)}, bf16[2,24]{1,0:T(2,128)(2,1)}, u32[]{:S(2)}) copy-start(bf16[2,24]{1,0:T(2,128)(2,1)} %param.35) | copy-start | bytes 292
  102.4 162.9 %copy-start.73 = (bf16[2,24]{1,0:T(2,128)(2,1)S(1)}, bf16[2,24]{1,0:T(2,128)(2,1)}, u32[]{:S(2)}) copy-start(bf16[2,24]{1,0:T(2,128)(2,1)} %param.36) | copy-start | bytes 292
  102.4 201.2 %copy-start.76 = (s32[32]{0:T(128)S(1)}, s32[32]{0:T(128)}, u32[]{:S(2)}) copy-start(s32[32]{0:T(128)} %param.28) | copy-start | bytes 388
  322.5 67.6 %copy-start.59 = (f32[768]{0:T(1024)S(1)}, f32[768]{0:T(1024)}, u32[]{:S(2)}) copy-start(f32[768]{0:T(1024)} %get-tuple-element.691) | copy-start | bytes 9220
  397.1 37.1 %copy-start.25 = (f32[1024,768]{0,1:T(8,128)S(1)}, f32[1024,768]{0,1:T(8,128)}, u32[]{:S(2)}) copy-start(f32[1024,768]{0,1:T(8,128)} %copy-done.24) | copy-start | bytes 9437188
  397.1 37.1 %copy-start.58 = (f32[768]{0:T(1024)S(1)}, f32[768]{0:T(1024)}, u32[]{:S(2)}) copy-start(f32[768]{0:T(1024)} %get-tuple-element.690) | copy-start | bytes 9220
  596.9 40.3 %copy-start.16 = (f32[1024,768]{0,1:T(8,128)S(1)}, f32[1024,768]{0,1:T(8,128)}, u32[]{:S(2)}) copy-start(f32[1024,768]{0,1:T(8,128)} %copy-done.15) | copy-start | bytes 9437188
  596.9 40.3 %copy-start.55 = (f32[768]{0:T(1024)S(1)}, f32[768]{0:T(1024)}, u32[]{:S(2)}) copy-start(f32[768]{0:T(1024)} %get-tuple-element.692) | copy-start | bytes 9220
  665.1 340.0 %reduce-scatter.9.cloned.1.call-start = ((), (), s32[]{:S(2)}) async-start(), calls=%async_computation.10 | async-start | bytes 9732096 | tf_op jit(solution)/shard_map/reduce_scatter | solution.py:407
  667.0 20.4 %copy-start.27 = (f32[1024,768]{0,1:T(8,128)S(1)}, f32[1024,768]{0,1:T(8,128)}, u32[]{:S(2)}) copy-start(f32[1024,768]{0,1:T(8,128)} %copy-done.26) | copy-start | bytes 9437188
  706.1 374.5 %reduce-scatter.7.cloned.1.call-start = ((), (), s32[]{:S(2)}) async-start(), calls=%async_computation.9 | async-start | bytes 9732096 | tf_op jit(solution)/shard_map/reduce_scatter | solution.py:406
  899.3 12.5 %copy-start.6 = (bf16[512,768]{0,1:T(8,128)(2,1)S(1)}, bf16[512,768]{0,1:T(8,128)(2,1)}, u32[]{:S(2)}) copy-start(bf16[512,768]{0,1:T(8,128)(2,1)} %copy.234) | copy-start | bytes 2359300 | tf_op jit(solution)/shard_map/while/body/eval_jaxpr/while
  929.0 17.4 %copy-start.18 = (bf16[1024,768]{1,0:T(8,128)(2,1)}, bf16[1024,768]{1,0:T(8,128)(2,1)S(1)}, u32[]{:S(2)}) copy-start(bf16[1024,768]{1,0:T(8,128)(2,1)S(1)} %copy.172) | copy-start | bytes 4718596
  997.2 83.5 %copy-start.20 = (f32[4,24,768]{2,1,0:T(8,128)S(1)}, f32[4,24,768]{2,1,0:T(8,128)}, u32[]{:S(2)}) copy-start(f32[4,24,768]{2,1,0:T(8,128)} %param.30) | copy-start | bytes 884740
  997.2 84.6 %copy-start.68 = (f32[24]{0:T(128)S(1)}, f32[24]{0:T(128)}, u32[]{:S(2)}) copy-start(f32[24]{0:T(128)} %copy-done.67) | copy-start | bytes 292
  997.2 86.4 %copy-start.66 = (f32[96]{0:T(128)S(1)}, f32[96]{0:T(128)}, u32[]{:S(2)}) copy-start(f32[96]{0:T(128)} %copy-done.65) | copy-start | bytes 1156
  997.2 88.2 %copy-start.40 = (f32[4,24]{1,0:T(4,128)S(1)}, f32[4,24]{1,0:T(4,128)}, u32[]{:S(2)}) copy-start(f32[4,24]{1,0:T(4,128)} %copy-done.39) | copy-start | bytes 1156
  (68 other events, 385.6 us)
Sparse Core Ops, SparseCore 0:
  11.0 66.6 all-gather.14
  80.6 62.9 all-gather.20
  146.5 62.5 all-gather.22
  212.4 62.5 all-gather.12
  278.3 62.4 all-gather.16
  344.2 62.4 all-gather.18
  665.2 133.0 reduce-scatter.10
  805.2 134.7 reduce-scatter.8
  945.9 134.7 reduce-scatter.6
where the time goes:
time: 1100 us; the launch traced here: 1090 us
  matrix products  491 us (45%)
  blocking collectives  309 us (28%)
  local copies, waits for them, and re-layouts  100 us (9%)
  other arithmetic  84.5 us (8%)
  waiting for transfers between devices  76.7 us (7%)
  between operations  20.6 us (2%)
  loops' own time  12.2 us (1%)
    dot_general x8, matrix products, project(): lax.dot_general(inputs, weight, (((1,), (1,)), ((), ())), preferred_eleme...  112 us
    sub x2, matrix products, attend_one_block(): grad_probs - weighted  80.3 us
    reduce_scatter x1, waiting for transfers between devices, on_device(): lax.psum_scatter(attn_weight_grad, ('dp', 'shard'), scatter_dimension=1,...  74.4 us
    all_gather x1, blocking collectives, on_device(): lax.all_gather(teacher_biases, ('dp', 'shard'), axis=1, tiled=True)  44 us
    all_gather x1, blocking collectives, on_device(): lax.all_gather(teacher_gains, ('dp', 'shard'), axis=1, tiled=True)  40.6 us
    psum x1, blocking collectives, on_device(): loss = lax.psum(local_loss, ('dp', 'shard'))  38.1 us
    unnamed x1, blocking collectives  37.8 us
    all_gather x1, blocking collectives, on_device(): lax.all_gather(norm_gains, ('dp', 'shard'), axis=1, tiled=True)  37.8 us
  transfers between devices with their start and end apart: 9, of which 1 were waited for; matrix products, arithmetic and copies ran while one was open for 58% of the time, Pallas kernels for 0%

commit v1 on v0

--- a/solution.py
+++ b/solution.py
@@ -208,6 +208,38 @@
         key_acc.reshape(SEQ_LEN, D),
         value_acc.reshape(SEQ_LEN, D),
     )
+
+
+def device_count():
+    return lax.axis_size(("dp", "shard"))
+
+
+def by_owner(rows):
+    return rows.reshape(rows.shape[0], device_count(), -1).transpose(1, 0, 2).reshape(device_count(), -1)
+
+
+def gather_layer(attn, up, down, bias, up_bias, gain, shift):
+    count, narrow, wide = device_count(), bias.shape[1], up.shape[0]
+    small = jnp.concatenate([bias.reshape(-1), up_bias, gain.reshape(-1), shift.reshape(-1)])
+    small = jnp.pad(small, (0, 8 * D - small.shape[0])).reshape(8, D)
+    block = jnp.concatenate([attn.reshape(-1, D), up, down.reshape(-1, D), small], axis=0)
+    every = lax.all_gather(block, ("dp", "shard"), axis=0, tiled=False)
+    at = 4 * narrow
+    attn_all = every[:, :at].reshape(count, 4, narrow, D).transpose(1, 0, 2, 3).reshape(4, D, D)
+    up_all = every[:, at : at + wide].reshape(-1, D)
+    down_all = every[:, at + wide : at + 2 * wide].reshape(D, -1)
+    flat = every[:, at + 2 * wide :].reshape(count, -1)
+
+    def spread(start, rows, width):
+        part = flat[:, start : start + rows * width].reshape(count, rows, width)
+        return part.transpose(1, 0, 2).reshape(rows, count * width)
+
+    start = 5 * narrow
+    bias_all = spread(0, 5, narrow)
+    up_bias_all = spread(start, 1, wide)[0]
+    gain_all = spread(start + wide, 2, narrow)
+    shift_all = spread(start + wide + 2 * narrow, 2, narrow)
+    return attn_all, up_all, down_all, bias_all, up_bias_all, gain_all, shift_all
 
 
 def by_sequence(array):
@@ -245,27 +277,17 @@
     pair_norm = HEADS * jnp.sum(live_float * live_float)
     positions = jnp.arange(SEQ_LEN, dtype=jnp.int32)
     row_live = (positions[None, :] < own_lengths[:, None]).reshape(rows)
-    student = (
-        lax.all_gather(binarize(attn_latent), ("dp", "shard"), axis=1, tiled=True),
-        lax.all_gather(binarize(up_latent), ("dp", "shard"), axis=0, tiled=True),
-        lax.all_gather(binarize(down_latent), ("dp", "shard"), axis=0, tiled=True),
-        lax.all_gather(biases, ("dp", "shard"), axis=1, tiled=True),
-        lax.all_gather(up_bias, ("dp", "shard"), axis=0, tiled=True),
-        lax.all_gather(norm_gains, ("dp", "shard"), axis=1, tiled=True),
-        lax.all_gather(norm_shifts, ("dp", "shard"), axis=1, tiled=True),
+    student = gather_layer(
+        binarize(attn_latent), binarize(up_latent), binarize(down_latent),
+        biases, up_bias, norm_gains, norm_shifts,
     )
     attn_w, up_w, down_w, bias_w, up_b, gain_w, shift_w = student
     bias_float = bias_w.astype(jnp.float32)
     gain_float = gain_w.astype(jnp.float32)
     shift_float = shift_w.astype(jnp.float32)
-    teacher = (
-        lax.all_gather(teacher_attn, ("dp", "shard"), axis=1, tiled=True),
-        lax.all_gather(teacher_up, ("dp", "shard"), axis=0, tiled=True),
-        lax.all_gather(teacher_down, ("dp", "shard"), axis=0, tiled=True),
-        lax.all_gather(teacher_biases, ("dp", "shard"), axis=1, tiled=True),
-        lax.all_gather(teacher_up_bias, ("dp", "shard"), axis=0, tiled=True),
-        lax.all_gather(teacher_gains, ("dp", "shard"), axis=1, tiled=True),
-        lax.all_gather(teacher_shifts, ("dp", "shard"), axis=1, tiled=True),
+    teacher = gather_layer(
+        teacher_attn, teacher_up, teacher_down,
+        teacher_biases, teacher_up_bias, teacher_gains, teacher_shifts,
     )
     teach_attn, teach_up, teach_down, teach_bias, teach_up_bias, teach_gain, teach_shift = teacher
     teach_bias_float = teach_bias.astype(jnp.float32)
@@ -338,12 +360,7 @@
     result = second_normed * gain_float[1] + shift_float[1]
     gap = jnp.where(row_live[:, None], result - teach_out, 0.0)
     local_loss = jnp.sum(gap * gap) / (D * token_norm) + jnp.sum(squares) / pair_norm
-    loss = lax.psum(local_loss, ("dp", "shard"))
-    back_attn, back_up, back_down = (
-        lax.all_gather(binarize(attn_latent), ("dp", "shard"), axis=1, tiled=True),
-        lax.all_gather(binarize(up_latent), ("dp", "shard"), axis=0, tiled=True),
-        lax.all_gather(binarize(down_latent), ("dp", "shard"), axis=0, tiled=True),
-    )
+    back_attn, back_up, back_down = attn_w, up_w, down_w
     grad_out = cotangent.astype(jnp.float32) + gap * (2.0 * hidden_weight)
     gain_two = jnp.sum(grad_out * second_normed, axis=0)
     shift_two = jnp.sum(grad_out, axis=0)
@@ -402,16 +419,35 @@
     bias_terms = jnp.concatenate([qkv_bias_grad, out_bias_grad[None], down_bias_grad[None]], axis=0)
     gain_terms = jnp.stack([gain_one, gain_two])
     shift_terms = jnp.stack([shift_one, shift_two])
-    summed = (
-        lax.psum_scatter(attn_weight_grad, ("dp", "shard"), scatter_dimension=1, tiled=True),
-        lax.psum_scatter(up_weight_grad, ("dp", "shard"), scatter_dimension=0, tiled=True),
-        lax.psum_scatter(down_weight_grad, ("dp", "shard"), scatter_dimension=0, tiled=True),
-        lax.psum_scatter(bias_terms, ("dp", "shard"), scatter_dimension=1, tiled=True),
-        lax.psum_scatter(up_bias_grad, ("dp", "shard"), scatter_dimension=0, tiled=True),
-        lax.psum_scatter(gain_terms, ("dp", "shard"), scatter_dimension=1, tiled=True),
-        lax.psum_scatter(shift_terms, ("dp", "shard"), scatter_dimension=1, tiled=True),
-    )
-    attn_total, up_total, down_total, bias_total, up_bias_total, gain_total, shift_total = summed
+    small = jnp.concatenate(
+        [
+            by_owner(bias_terms), by_owner(up_bias_grad[None]),
+            by_owner(gain_terms), by_owner(shift_terms),
+            jnp.full((device_count(), 1), local_loss, jnp.float32),
+        ],
+        axis=1,
+    )
+    small = jnp.pad(small, ((0, 0), (0, 8 * D - small.shape[1]))).reshape(-1, 8, D)
+    packed = jnp.concatenate(
+        [
+            attn_weight_grad.reshape(4, device_count(), -1, D).transpose(1, 0, 2, 3).reshape(device_count(), -1, D),
+            up_weight_grad.reshape(device_count(), -1, D),
+            small,
+        ],
+        axis=1,
+    )
+    total = lax.psum_scatter(packed, ("dp", "shard"), scatter_dimension=0, tiled=True)[0]
+    down_total = lax.psum_scatter(down_weight_grad, ("dp", "shard"), scatter_dimension=0, tiled=True)
+    attn_rows, up_rows = attn_latent.shape[0] * attn_latent.shape[1], up_latent.shape[0]
+    attn_total = total[:attn_rows].reshape(attn_latent.shape)
+    up_total = total[attn_rows : attn_rows + up_rows]
+    flat = total[attn_rows + up_rows :].reshape(-1)
+    narrow = biases.shape[1]
+    bias_total, flat = flat[: 5 * narrow].reshape(5, narrow), flat[5 * narrow :]
+    up_bias_total, flat = flat[:up_rows], flat[up_rows:]
+    gain_total, flat = flat[: 2 * narrow].reshape(2, narrow), flat[2 * narrow :]
+    shift_total, flat = flat[: 2 * narrow].reshape(2, narrow), flat[2 * narrow :]
+    loss = flat[0]
     return (
         result.astype(jnp.bfloat16),
         loss,

time: 1100 us -> 1180 us (1.073)
  blocking collectives: 309 us -> 0 us
  waiting for transfers between devices: 76.7 us -> 366 us
  local copies, waits for them, and re-layouts: 100 us -> 186 us
    all_gather x6 -> x0, blocking collectives: 233 us -> none  [the longest x1 44 us: on_device(): lax.all_gather(teacher_biases, ('dp', 'shard'), axis=1, tiled=True)]
    all_gather x6 -> x2, waiting for transfers between devices: 0.08 us -> 174 us  [gather_layer(): every = lax.all_gather(block, ('dp', 'shard'), axis=0, tiled=False)]
    reduce_scatter x2 -> x1, waiting for transfers between devices: 74.4 us -> 192 us  [on_device(): lax.psum_scatter(packed, ('dp', 'shard'), scatter_dimension=0, tiled=True)]
    psum x1 -> x0, blocking collectives: 38.1 us -> none  [on_device(): loss = lax.psum(local_loss, ('dp', 'shard'))]
    unnamed x1 -> x0, blocking collectives: 37.8 us -> none
    slice x1 -> x21, local copies, waits for them, and re-layouts: 0.75 us -> 37.2 us  [the longest x2 22.3 us: gather_layer(): up_all = every[:, at:at + wide].reshape(-1, D)]
    reshape x1 -> x16, local copies, waits for them, and re-layouts: 0.01 us -> 23.1 us  [the longest x2 17.1 us: gather_layer(): down_all = every[:, at + wide:at + 2 * wide].reshape(D, -1)]
    convert_element_type x8 -> x10, local copies, waits for them, and re-layouts: 0.76 us -> 13.2 us  [the longest x2 2.78 us: on_device(): teach_shift[0].astype(jnp.float32)]
  transfers between devices with their start and end apart: 9 -> 4, of which waited for: 1 -> 3; matrix products, arithmetic and copies ran while one was open for 58% -> 26% of each run, Pallas kernels for 0% -> 0%
where the time goes in v1:
time: 1180 us; the launch traced here: 1170 us
  matrix products  490 us (42%)
  waiting for transfers between devices  366 us (31%)
  local copies, waits for them, and re-layouts  186 us (16%)
  other arithmetic  96.3 us (8%)
  between operations  21 us (2%)
  loops' own time  13 us (1%)
    reduce_scatter x1, waiting for transfers between devices, on_device(): lax.psum_scatter(packed, ('dp', 'shard'), scatter_dimension=0, tiled=True)  192 us
    all_gather x2, waiting for transfers between devices, gather_layer(): every = lax.all_gather(block, ('dp', 'shard'), axis=0, tiled=False)  174 us
    dot_general x8, matrix products, project(): lax.dot_general(inputs, weight, (((1,), (1,)), ((), ())), preferred_eleme...  107 us
    sub x2, matrix products, attend_one_block(): grad_probs - weighted  83.3 us
    dot_general x4, matrix products, outer_rows(): lax.dot_general(left, right, (((0,), (0,)), ((), ())), preferred_element_...  31.1 us
    unnamed x202, local copies, waits for them, and re-layouts  28.3 us
    dot_general x2, matrix products, student_one_block(): jnp.einsum('qhe,khe->hqk', teacher_block, teacher_keys, preferred_element...  27.5 us
    dot_general x2, matrix products, attend_one_block(): jnp.einsum('hqk,qhe->khe', probs.astype(jnp.bfloat16), grad_block, prefer...  27.1 us
  transfers between devices with their start and end apart: 4, of which 3 were waited for; matrix products, arithmetic and copies ran while one was open for 26% of the time, Pallas kernels for 0%

profile of v1, /device:TPU:0, one launch (start us, length us, event | category | flops | bytes accessed | tf_op | source)
XLA Modules:
  0.0 1171.7 jit_solution(8273793929377567056)
XLA Ops:
  39.1 81.9 %all-gather.7.cloned.1.call-done = bf16[9472,768]{1,0:T(8,128)(2,1)} async-done(((bf16[296,768]{1,0:T(8,128)(2,1)}), bf16[9472,768]{1,0:T(8,128)(2,1)}) %all-gather.7.cloned.1.call-update) | async-done | bytes 14549008 | tf_op jit(solution)/shard_map/all_gather | solution.py:226
  124.9 11.2 fusion.139
  136.1 91.6 %all-gather.5.cloned.1.call-done = bf16[9472,768]{1,0:T(8,128)(2,1)} async-done(((bf16[296,768]{1,0:T(8,128)(2,1)}), bf16[9472,768]{1,0:T(8,128)(2,1)}) %all-gather.5.cloned.1.call-update) | async-done | bytes 14549008 | tf_op jit(solution)/shard_map/all_gather | solution.py:226
  228.7 11.1 fusion.140
  302.0 67.5 %while.76 = (s32[]{:T(128)}, bf16[2,512,768]{2,1,0:T(8,128)(2,1)}, s32[2]{0:T(128)S(1)}, bf16[1024,768]{0,1:T(8,128)(2,1)S(1)}, bf16[1024,12,64]{0,2,1:T(8,128)(...) while((s32[]{:T(128)}, bf16[2,512,768]{2,1,0:T(8,128)(2,1)}, s32[2]{0:T(128)S(1)}, ...), condition=%wide.region_15.16_spmd.clone.clone, body=%wide.region_12.15_spmd.clone.sunk.clone | while | flops 1648363520 | bytes 59820172 | solution.py:100
  306.6 13.3 %fusion.280 = (f32[12,512]{1,0:T(8,128)S(1)}, f32[12,512,1024]{2,1,0:T(8,128)}) fusion(pred[1024]{0:T(1024)(128)(4,1)S(1)} %iota_compare_fusion.11, bf16[512,12,64]{0,2,1:T(8,128)(2,1)} %bitcast.297, bf16[1024,12,64]{0,2,1:T(8,128)(2,1)S(1)} %get-tuple-element.1099), kind=kOutput, calls=%fused_computation.269.clone.1.clone | convolution fusion | flops 830473216 | bytes 27550720 | tf_op jit(solution)/shard_map/while/body/eval_jaxpr/while/body/eval_jaxpr/sub | solution.py:72
  319.9 11.6 fusion.281
  340.3 13.3 %fusion.280 = (f32[12,512]{1,0:T(8,128)S(1)}, f32[12,512,1024]{2,1,0:T(8,128)}) fusion(pred[1024]{0:T(1024)(128)(4,1)S(1)} %iota_compare_fusion.11, bf16[512,12,64]{0,2,1:T(8,128)(2,1)} %bitcast.297, bf16[1024,12,64]{0,2,1:T(8,128)(2,1)S(1)} %get-tuple-element.1099), kind=kOutput, calls=%fused_computation.269.clone.1.clone | convolution fusion | flops 830473216 | bytes 27550720 | tf_op jit(solution)/shard_map/while/body/eval_jaxpr/while/body/eval_jaxpr/sub | solution.py:72
  353.6 11.6 fusion.281
  387.4 123.5 %while.77 = (s32[]{:T(128)}, f32[2,512,768]{2,1,0:T(8,128)}, f32[2,12,512]{2,1,0:T(8,128)}, f32[2]{0:T(128)S(1)}, s32[2]{0:T(128)S(1)}, /*index=5*/bf16[1024,768...) while((s32[]{:T(128)}, f32[2,512,768]{2,1,0:T(8,128)}, ...), condition=%wide.region_7.8_spmd.clone.clone.clone, body=%wide.region_3.7_spmd.clone.clone.sunk.clone | while | flops 2529685504 | bytes 125516016 | solution.py:136
  394.7 10.2 select_reduce_fusion.3
  404.9 13.8 %multiply_reduce_fusion.19 = f32[]{:T(128)} fusion(f32[12,512,1024]{2,1,0:T(8,128)} %get-tuple-element.997, pred[512,1024]{1,0:T(8,128)(4,1)S(1)} %broadcast_and_fusion.6, bf16[512,12,64]{0,2,1:T(8,128)(2,1)S(1)} %bitcast.299, bf16[1024,12,64]{0,2,1:T(8,128)(2,1)S(1)} %get-tuple-element.1080), kind=kOutput, calls=%fused_computation.18.clone.1.clone | convolution fusion | flops 843055104 | bytes 28049412 | tf_op jit(solution)/shard_map/while/body/eval_jaxpr/while/body/eval_jaxpr/qhe,khe->hqk/dot_general | solution.py:121
  419.4 11.3 fusion.287
  430.8 12.3 %fusion.288 = f32[12,512,64]{1,2,0:T(8,128)} fusion(bf16[1024,12,64]{0,2,1:T(8,128)(2,1)S(1)} %copy-done.35, f32[12,512,1024]{2,1,0:T(8,128)} %get-tuple-element.997, f32[12,512]{1,0:T(8,128)S(1)} %fusion.287, f32[12,512]{1,0:T(8,128)S(1)} %get-tuple-element.998, pred[1024]{0:T(1024)(128)(4,1)S(1)} %iota_compare_fusion.12), kind=kOutput, calls=%fused_computation.23.clone.1.clone | convolution fusion | flops 836763648 | bytes 28361728 | tf_op jit(solution)/shard_map/while/body/eval_jaxpr/while/body/eval_jaxpr/hqk,khe->qhe/dot_general | solution.py:127
  456.2 10.2 select_reduce_fusion.3
  466.4 13.8 %multiply_reduce_fusion.19 = f32[]{:T(128)} fusion(f32[12,512,1024]{2,1,0:T(8,128)} %get-tuple-element.997, pred[512,1024]{1,0:T(8,128)(4,1)S(1)} %broadcast_and_fusion.6, bf16[512,12,64]{0,2,1:T(8,128)(2,1)S(1)} %bitcast.299, bf16[1024,12,64]{0,2,1:T(8,128)(2,1)S(1)} %get-tuple-element.1080), kind=kOutput, calls=%fused_computation.18.clone.1.clone | convolution fusion | flops 843055104 | bytes 28049412 | tf_op jit(solution)/shard_map/while/body/eval_jaxpr/while/body/eval_jaxpr/qhe,khe->hqk/dot_general | solution.py:121
  480.9 11.3 fusion.287
  492.3 12.3 %fusion.288 = f32[12,512,64]{1,2,0:T(8,128)} fusion(bf16[1024,12,64]{0,2,1:T(8,128)(2,1)S(1)} %copy-done.35, f32[12,512,1024]{2,1,0:T(8,128)} %get-tuple-element.997, f32[12,512]{1,0:T(8,128)S(1)} %fusion.287, f32[12,512]{1,0:T(8,128)S(1)} %get-tuple-element.998, pred[1024]{0:T(1024)(128)(4,1)S(1)} %iota_compare_fusion.12), kind=kOutput, calls=%fused_computation.23.clone.1.clone | convolution fusion | flops 836763648 | bytes 28361728 | tf_op jit(solution)/shard_map/while/body/eval_jaxpr/while/body/eval_jaxpr/hqk,khe->qhe/dot_general | solution.py:127
  537.0 34.2 %fusion.79.clone.4 = bf16[1024,3072]{1,0:T(8,128)(2,1)S(1)} fusion(f32[3072]{0:T(1024)S(1)} %copy-done.64, bf16[3072,768]{1,0:T(8,128)(2,1)} %bitcast.317, f32[1024,768]{0,1:T(8,128)S(1)} %copy-done.22, f32[768]{0:T(1024)S(1)} %copy-done.71, f32[768]{0:T(1024)S(1)} %copy-done.72, f32[1024]{0:T(1024)S(1)} %copy-done.79, ...), kind=kOutput, calls=%fused_computation.72.clone.clone.clone.clone.clone.clone.1 | convolution fusion | flops 5043388416 | bytes 14182400 | tf_op jit(solution)/shard_map/dot_general | solution.py:21
  577.1 44.7 %fusion.44 = (f32[1024,3072]{1,0:T(8,128)}, f32[1024,3072]{1,0:T(8,128)}) fusion(f32[3072]{0:T(1024)S(1)} %copy-done.63, f32[]{:T(128)} %bitcast.29, bf16[3072,768]{1,0:T(8,128)(2,1)} %bitcast.315, f32[]{:T(128)} %bitcast.30, f32[768]{0:T(1024)S(1)} %copy-done.69, f32[768]{0:T(1024)S(1)} %copy-done.51, f32[1024]{0:T(1024)S(1)} %add_rsqrt_fusion.3, ...), kind=kOutput, calls=%fused_computation.69 | convolution fusion | flops 5044961280 | bytes 33056776 | tf_op jit(solution)/shard_map/dot_general | solution.py:21
  639.1 12.0 %fusion.76 = f32[768,3072]{1,0:T(8,128)} fusion(f32[1024,3072]{1,0:T(8,128)} %get-tuple-element.740, f32[]{:T(128)} %bitcast.29, f32[1024,768]{0,1:T(8,128)S(1)} %get-tuple-element.689), kind=kOutput, calls=%fused_computation.159 | convolution fusion | flops 4838916096 | bytes 25165828 | tf_op jit(solution)/shard_map/dot_general | solution.py:27
  651.1 18.3 %convert_reduce_fusion = (f32[3072]{0:T(1024)}, bf16[1024,3072]{1,0:T(8,128)(2,1)S(1)}) fusion(f32[1024,3072]{1,0:T(8,128)} %get-tuple-element.741, f32[3072]{0:T(1024)S(1)} %copy-done.63, f32[1024,3072]{1,0:T(8,128)} %get-tuple-element.740, bf16[768,3072]{1,0:T(8,128)(2,1)} %reshape.615, f32[1024,768]{0,1:T(8,128)} %copy-done.25), kind=kOutput, calls=%fused_computation.79 | convolution fusion | flops 4882953216 | bytes 39346176 | tf_op jit(solution)/shard_map/dot_general | solution.py:371
  672.1 10.2 multiply_reduce_fusion.4
  689.0 210.2 %while.78 = (s32[]{:T(128)}, f32[1024,12,64]{0,2,1:T(8,128)}, f32[1024,12,64]{0,2,1:T(8,128)}, bf16[2,512,768]{2,1,0:T(8,128)(2,1)}, s32[2]{0:T(128)S(1)}, /*ind...) while((s32[]{:T(128)}, f32[1024,12,64]{0,2,1:T(8,128)}, ...), condition=%wide.region_27.28_spmd.clone.clone.clone.clone, body=%wide.region_25.27_spmd.clone.clone.clone.sunk.clone | while | flops 5768225792 | bytes 204051712 | solution.py:203
  698.8 11.1 fusion.305
  709.8 11.0 fusion.306
  720.9 41.6 %add_convert_fusion.6 = bf16[12,512,1024]{2,1,0:T(8,128)(2,1)} fusion(f32[12,512,1024]{2,1,0:T(8,128)} %fusion.305, f32[12,512,1024]{2,1,0:T(8,128)} %fusion.306, f32[]{:T(128)} %get-tuple-element.1143, f32[12,512]{1,0:T(8,128)S(1)} %dynamic-slice_bitcast_fusion.3, pred[512,1024]{1,0:T(8,128)(4,1)} %broadcast_and_fusion.7, ...), kind=kOutput, calls=%fused_computation.34.clone.1.clone | convolution fusion | flops 1711283200 | bytes 65823748 | tf_op jit(solution)/shard_map/while/body/eval_jaxpr/while/body/eval_jaxpr/sub | solution.py:181
  762.5 13.2 %bitcast_add_fusion.7 = f32[1024,12,64]{0,2,1:T(8,128)} fusion(f32[1024,12,64]{0,2,1:T(8,128)} %get-tuple-element.1118, bf16[512,12,64]{0,2,1:T(8,128)(2,1)S(1)} %bitcast.295, f32[12,512,1024]{2,1,0:T(8,128)} %fusion.306, f32[12,512]{1,0:T(8,128)S(1)} %dynamic-slice_bitcast_fusion.3, pred[1024]{0:T(1024)(128)(4,1)S(1)} %iota_compare_fusion.13, ...), kind=kOutput, calls=%fused_computation.46.clone.1.clone | convolution fusion | flops 832045056 | bytes 32269312 | tf_op jit(solution)/shard_map/while/body/eval_jaxpr/while/body/eval_jaxpr/hqk,qhe->khe/dot_general | solution.py:193
  804.0 10.2 fusion.305
  824.4 41.6 %add_convert_fusion.6 = bf16[12,512,1024]{2,1,0:T(8,128)(2,1)} fusion(f32[12,512,1024]{2,1,0:T(8,128)} %fusion.305, f32[12,512,1024]{2,1,0:T(8,128)} %fusion.306, f32[]{:T(128)} %get-tuple-element.1143, f32[12,512]{1,0:T(8,128)S(1)} %dynamic-slice_bitcast_fusion.3, pred[512,1024]{1,0:T(8,128)(4,1)} %broadcast_and_fusion.7, ...), kind=kOutput, calls=%fused_computation.34.clone.1.clone | convolution fusion | flops 1711283200 | bytes 65823748 | tf_op jit(solution)/shard_map/while/body/eval_jaxpr/while/body/eval_jaxpr/sub | solution.py:181
  866.0 13.9 %bitcast_add_fusion.7 = f32[1024,12,64]{0,2,1:T(8,128)} fusion(f32[1024,12,64]{0,2,1:T(8,128)} %get-tuple-element.1118, bf16[512,12,64]{0,2,1:T(8,128)(2,1)S(1)} %bitcast.295, f32[12,512,1024]{2,1,0:T(8,128)} %fusion.306, f32[12,512]{1,0:T(8,128)S(1)} %dynamic-slice_bitcast_fusion.3, pred[1024]{0:T(1024)(128)(4,1)S(1)} %iota_compare_fusion.13, ...), kind=kOutput, calls=%fused_computation.46.clone.1.clone | convolution fusion | flops 832045056 | bytes 32269312 | tf_op jit(solution)/shard_map/while/body/eval_jaxpr/while/body/eval_jaxpr/hqk,qhe->khe/dot_general | solution.py:193
  964.2 192.4 %reduce-scatter.3.cloned.1.call-done = f32[1,200,768]{2,1,0:T(8,128)} async-done(((f32[32,200,768]{2,1,0:T(8,128)}), f32[1,200,768]{2,1,0:T(8,128)}) %reduce-scatter.3.cloned.1.call-update) | async-done | bytes 614416 | tf_op jit(solution)/shard_map/reduce_scatter | solution.py:439
  (445 shorter events, 342.5 us)
Async XLA Ops:
  7.2 17.2 %copy-start.68 = (f32[4]{0:T(128)S(1)}, f32[4]{0:T(128)}, u32[]{:S(2)}) copy-start(f32[4]{0:T(128)} %param.29) | copy-start | bytes 52
  7.2 20.4 %copy-start.28 = (bf16[1024,768]{1,0:T(8,128)(2,1)S(1)}, bf16[1024,768]{1,0:T(8,128)(2,1)}, u32[]{:S(2)}) copy-start(bf16[1024,768]{1,0:T(8,128)(2,1)} %param.25) | copy-start | bytes 4718596
  7.2 22.0 %copy-start.29 = (bf16[1024,768]{1,0:T(8,128)(2,1)S(1)}, bf16[1024,768]{1,0:T(8,128)(2,1)}, u32[]{:S(2)}) copy-start(bf16[1024,768]{1,0:T(8,128)(2,1)} %param.27) | copy-start | bytes 4718596
  7.2 113.9 %all-gather.7.cloned.1.call-start = ((), (), s32[]{:S(2)}) async-start(), calls=%async_computation.5 | async-start | bytes 15003648 | tf_op jit(solution)/shard_map/all_gather | solution.py:226
  13.3 214.4 %all-gather.5.cloned.1.call-start = ((), (), s32[]{:S(2)}) async-start(), calls=%async_computation.4 | async-start | bytes 15003648 | tf_op jit(solution)/shard_map/all_gather | solution.py:226
  24.3 937.0 %reduce-scatter.5.cloned.1.call-start = ((), (), s32[]{:S(2)}) async-start(), calls=%async_computation.3 | async-start | bytes 9732096 | tf_op jit(solution)/shard_map/reduce_scatter | solution.py:440
  302.0 67.5 %copy-start.78 = (f32[768]{0:T(1024)S(1)}, f32[768]{0:T(1024)}, u32[]{:S(2)}) copy-start(f32[768]{0:T(1024)} %add.287) | copy-start | bytes 9220
  517.8 164.6 %copy-start.42 = (f32[1024]{0:T(1024)}, f32[1024]{0:T(1024)S(1)}, u32[]{:S(2)}) copy-start(f32[1024]{0:T(1024)S(1)} %broadcast_multiply_fusion.7) | copy-start | bytes 12292
  519.8 162.6 %copy-start.55 = (f32[1024]{0:T(1024)}, f32[1024]{0:T(1024)S(1)}, u32[]{:S(2)}) copy-start(f32[1024]{0:T(1024)S(1)} %add_rsqrt_fusion.3) | copy-start | bytes 12292
  537.0 34.2 %copy-start.17 = (bf16[768,3072]{1,0:T(8,128)(2,1)S(1)}, bf16[768,3072]{1,0:T(8,128)(2,1)}, u32[]{:S(2)}) copy-start(bf16[768,3072]{1,0:T(8,128)(2,1)} %reshape.620) | copy-start | bytes 14155780
  537.0 34.2 %copy-start.23 = (f32[1024,768]{0,1:T(8,128)S(1)}, f32[1024,768]{0,1:T(8,128)}, u32[]{:S(2)}) copy-start(f32[1024,768]{0,1:T(8,128)} %copy-done.21) | copy-start | bytes 9437188
  537.0 34.2 %copy-start.73 = (f32[768]{0:T(1024)S(1)}, f32[768]{0:T(1024)}, u32[]{:S(2)}) copy-start(f32[768]{0:T(1024)} %add.295) | copy-start | bytes 9220
  571.3 50.5 %slice-start = ((s8[4718592]{0:T(1024)(128)(4,1)}), s8[4194304]{0:T(1024)(128)(4,1)S(1)}, s32[]{:S(2)}) async-start(s8[4718592]{0:T(1024)(128)(4,1)} %bitcast.318), calls=%async_computation.6 | async-start | bytes 8388608
  577.1 44.7 %slice-start.1 = ((s8[4718592]{0:T(1024)(128)(4,1)}), s8[524288]{0:T(1024)(128)(4,1)S(1)}, s32[]{:S(2)}) async-start(s8[4718592]{0:T(1024)(128)(4,1)} %bitcast.318), calls=%async_computation.7 | async-start | bytes 1048576
  577.1 44.7 %copy-start.74 = (f32[768]{0:T(1024)S(1)}, f32[768]{0:T(1024)}, u32[]{:S(2)}) copy-start(f32[768]{0:T(1024)} %add.278) | copy-start | bytes 9220
  651.1 20.9 %copy-start.26 = (f32[1024,768]{0,1:T(8,128)S(1)}, f32[1024,768]{0,1:T(8,128)}, u32[]{:S(2)}) copy-start(f32[1024,768]{0,1:T(8,128)} %copy-done.25) | copy-start | bytes 9437188
  682.3 474.3 %reduce-scatter.3.cloned.1.call-start = ((), (), s32[]{:S(2)}) async-start(), calls=%async_computation.2 | async-start | bytes 20275200 | tf_op jit(solution)/shard_map/reduce_scatter | solution.py:439
  688.9 210.3 %copy-start.91 = (f32[2]{0:T(128)S(1)}, f32[2]{0:T(128)}, u32[]{:S(2)}) copy-start(f32[2]{0:T(128)} %copy-done.90) | copy-start | bytes 28
  688.9 211.6 %copy-start.65 = (f32[3072]{0:T(1024)S(1)}, f32[3072]{0:T(1024)}, u32[]{:S(2)}) copy-start(f32[3072]{0:T(1024)} %get-tuple-element.749) | copy-start | bytes 36868
  688.9 211.6 %copy-start.77 = (f32[768]{0:T(1024)S(1)}, f32[768]{0:T(1024)}, u32[]{:S(2)}) copy-start(f32[768]{0:T(1024)} %get-tuple-element.613) | copy-start | bytes 9220
  689.0 211.7 %copy-start.53 = (f32[768]{0:T(1024)S(1)}, f32[768]{0:T(1024)}, u32[]{:S(2)}) copy-start(f32[768]{0:T(1024)} %get-tuple-element.688) | copy-start | bytes 9220
  689.0 211.8 %copy-start.50 = (f32[768]{0:T(1024)S(1)}, f32[768]{0:T(1024)}, u32[]{:S(2)}) copy-start(f32[768]{0:T(1024)} %get-tuple-element.611) | copy-start | bytes 9220
  689.0 212.0 %copy-start.76 = (f32[768]{0:T(1024)S(1)}, f32[768]{0:T(1024)}, u32[]{:S(2)}) copy-start(f32[768]{0:T(1024)} %get-tuple-element.619) | copy-start | bytes 9220
  689.0 212.1 %copy-start.49 = (f32[768]{0:T(1024)S(1)}, f32[768]{0:T(1024)}, u32[]{:S(2)}) copy-start(f32[768]{0:T(1024)} %get-tuple-element.616) | copy-start | bytes 9220
  689.0 212.4 %copy-start.54 = (f32[768]{0:T(1024)S(1)}, f32[768]{0:T(1024)}, u32[]{:S(2)}) copy-start(f32[768]{0:T(1024)} %get-tuple-element.686) | copy-start | bytes 9220
  904.3 14.1 %copy-start.14 = (bf16[1024,768]{1,0:T(8,128)(2,1)}, bf16[1024,768]{1,0:T(8,128)(2,1)S(1)}, u32[]{:S(2)}) copy-start(bf16[1024,768]{1,0:T(8,128)(2,1)S(1)} %copy.158) | copy-start | bytes 4718596
  949.9 11.4 copy-start.18
  949.9 12.5 %copy-start.83 = (f32[24]{0:T(128)S(1)}, f32[24]{0:T(128)}, u32[]{:S(2)}) copy-start(f32[24]{0:T(128)} %copy-done.82) | copy-start | bytes 292
  959.6 200.2 %copy-start.19 = (f32[96,768]{1,0:T(8,128)S(1)}, f32[96,768]{1,0:T(8,128)}, u32[]{:S(2)}) copy-start(f32[96,768]{1,0:T(8,128)} %param.31) | copy-start | bytes 884740
  959.6 202.3 %copy-start.16 = (f32[4,24,768]{2,1,0:T(8,128)S(1)}, f32[4,24,768]{2,1,0:T(8,128)}, u32[]{:S(2)}) copy-start(f32[4,24,768]{2,1,0:T(8,128)} %param.30) | copy-start | bytes 884740
  959.6 202.4 %copy-start.45 = (f32[4,24]{1,0:T(4,128)S(1)}, f32[4,24]{1,0:T(4,128)}, u32[]{:S(2)}) copy-start(f32[4,24]{1,0:T(4,128)} %copy-done.44) | copy-start | bytes 1156
  959.6 203.3 %copy-start.81 = (f32[96]{0:T(128)S(1)}, f32[96]{0:T(128)}, u32[]{:S(2)}) copy-start(f32[96]{0:T(128)} %copy-done.80) | copy-start | bytes 1156
  (69 other events, 358.3 us)
Sparse Core Ops, SparseCore 0:
  13.4 107.6 all-gather.6
  124.5 103.0 all-gather.4
  682.4 133.6 reduce-scatter.4
  947.0 209.5 reduce-scatter.2

commit v2 on v0

v2 whole, which is shorter than its diff:
```python
import functools
import math

import jax
import jax.numpy as jnp
from jax import lax
from jax.experimental import pallas as pl
from jax.experimental.pallas import tpu as pltpu
from jax.sharding import PartitionSpec as P

D = 768
HEADS = 12
HEAD_DIM = 64
SEQ_LEN = 1024
AXES = ("dp", "shard")
MESH = pl.DeviceIdType.MESH
F32 = jnp.float32
BF16 = jnp.bfloat16

epsilon = 1e-05
masked_score = -1e30
hidden_weight = 0.25
saturation = 7.5
LANES = 128
log2e = math.log2(math.e)
scaling = HEAD_DIM ** (-0.5)
exponent = scaling * log2e
vmem_bytes = 60 * 1024 * 1024


def dot(left, right, left_dim, right_dim):
    return lax.dot_general(
        left, right, (((left_dim,), (right_dim,)), ((), ())), preferred_element_type=F32
    )


def outer_rows(left, right):
    return dot(left, right, 0, 0)


def binarize(latent):
    scale = jnp.mean(jnp.abs(latent), axis=-1, keepdims=True)
    return (scale * jnp.sign(latent)).astype(BF16)


def surrogate(latent):
    return jnp.mean(jnp.abs(latent), axis=-1, keepdims=True) * latent


def latent_grad(latent, grad):
    _, pull = jax.vjp(surrogate, latent)
    return pull(grad)[0]


def normalize(values):
    center = values - jnp.mean(values, axis=-1, keepdims=True)
    inverse = lax.rsqrt(jnp.mean(center * center, axis=-1, keepdims=True) + epsilon)
    return (center * inverse, inverse)


def norm_back(grad_norm, normed, inverse):
    return inverse * (
        grad_norm
        - jnp.mean(grad_norm, axis=-1, keepdims=True)
        - normed * jnp.mean(grad_norm * normed, axis=-1, keepdims=True)
    )


def whole(memory=pltpu.VMEM):
    return pl.BlockSpec(memory_space=memory)


def fixed(shape):
    return pl.BlockSpec(shape, lambda *_: (0,) * len(shape), pipeline_mode=pl.Buffered(1))


def columns(shape):
    return pl.BlockSpec(shape, lambda i: (0,) * (len(shape) - 1) + (i,))


def row_blocks(shape):
    return pl.BlockSpec(shape, lambda i: (i,) + (0,) * (len(shape) - 1))


def gather_kernel(count, shapes, chunks, depth, *refs):
    ins, outs = refs[:count], refs[count : 2 * count]
    line_send, line_recv, pair_send, pair_recv, own_sem = refs[2 * count :]
    dp, shard = lax.axis_index("dp"), lax.axis_index("shard")
    z, y = dp // 2, lax.rem(dp, 2)
    x, core = shard // 2, lax.rem(shard, 2)

    def device(z_at, y_at, x_at, core_at):
        return (z_at * 2 + y_at, x_at * 2 + core_at)

    above = device(jnp.minimum(z + 1, depth - 1), y, x, core)
    below = device(jnp.maximum(z - 1, 0), y, x, core)
    y_one, x_one = lax.rem(y + 1 - core, 2), lax.rem(x + core, 2)
    y_two, x_two = lax.rem(y + core, 2), lax.rem(x + 1 - core, 2)
    first, second = device(z, y_one, x_one, core), device(z, y_two, x_two, core)
    sibling = device(z, y, x, 1 - core)
    barrier = pltpu.get_barrier_semaphore()
    for partner in (first, second, sibling):
        pl.semaphore_signal(barrier, inc=1, device_id=partner, device_id_type=MESH)

    @pl.when(z < depth - 1)
    def _():
        pl.semaphore_signal(barrier, inc=1, device_id=above, device_id_type=MESH)

    @pl.when(z > 0)
    def _():
        pl.semaphore_signal(barrier, inc=1, device_id=below, device_id_type=MESH)

    pl.semaphore_wait(barrier, 3 + jnp.minimum(z, 1) + jnp.minimum(depth - 1 - z, 1))

    def slot(item, *index):
        return outs[item].at[((slice(None),) if shapes[item][0] > 1 else ()) + index]

    def line_copy(chunk, at, item, turn, upward):
        if upward:
            owner, target = jnp.maximum(z - (turn - 1), 0), above
        else:
            owner, target = jnp.minimum(z + (turn - 1), depth - 1), below
        block = slot(item, owner, y, x, core)
        return pltpu.make_async_remote_copy(
            src_ref=block,
            dst_ref=block,
            send_sem=line_send.at[chunk, at, turn - 1, int(upward)],
            recv_sem=line_recv.at[chunk, at, turn - 1, int(upward)],
            device_id=target,
            device_id_type=MESH,
        )

    def sends(turn, upward):
        if upward:
            return (z - (turn - 1) >= 0) & (z < depth - 1)
        return (z + (turn - 1) <= depth - 1) & (z > 0)

    def receives(turn, upward):
        return (z - turn >= 0) if upward else (z + turn <= depth - 1)

    def own_copy(chunk, at, item):
        return pltpu.make_async_copy(
            ins[item], slot(item, z, y, x, core), own_sem.at[chunk, at]
        )

    plans = (
        ((y, x), first),
        ((y, x), second),
        ((y_one, x_one), second),
        ((y, x), sibling),
        ((y_one, x_one), sibling),
        ((y_two, x_two), sibling),
        ((1 - y, 1 - x), sibling),
    )

    def pair_copy(chunk, at, item, plan):
        (y_at, x_at), target = plans[plan]
        block = slot(item, slice(None), y_at, x_at, core)
        return pltpu.make_async_remote_copy(
            src_ref=block,
            dst_ref=block,
            send_sem=pair_send.at[chunk, at, plan],
            recv_sem=pair_recv.at[chunk, at, plan],
            device_id=target,
            device_id_type=MESH,
        )

    def each(chunk, action):
        for at, item in enumerate(chunks[chunk]):
            action(at, item)

    def line_start(chunk, turn):
        for upward in (True, False):

            @pl.when(sends(turn, upward))
            def _():
                each(chunk, lambda at, item: line_copy(chunk, at, item, turn, upward).start())

    def line_received(chunk, turn):
        for upward in (True, False):

            @pl.when(receives(turn, upward))
            def _():
                each(chunk, lambda at, item: line_copy(chunk, at, item, turn, upward).wait_recv())

    def line_sent(chunk, turn):
        for upward in (True, False):

            @pl.when(sends(turn, upward))
            def _():
                each(chunk, lambda at, item: line_copy(chunk, at, item, turn, upward).wait_send())

    def start(chunk, *plan_list):
        for plan in plan_list:
            each(chunk, lambda at, item: pair_copy(chunk, at, item, plan).start())

    def received(chunk, *plan_list):
        for plan in plan_list:
            each(chunk, lambda at, item: pair_copy(chunk, at, item, plan).wait_recv())

    def stage(chunk, number):
        if number == 0:
            each(chunk, lambda at, item: own_copy(chunk, at, item).wait())
            line_start(chunk, 1)
        elif number < depth:
            line_received(chunk, number)
            if number < depth - 1:
                line_start(chunk, number + 1)
            else:
                start(chunk, 0, 1, 3)
        elif number == depth:
            received(chunk, 0)
            start(chunk, 2, 4)
        elif number == depth + 1:
            received(chunk, 1)
            start(chunk, 5)
        elif number == depth + 2:
            received(chunk, 2)
            start(chunk, 6)
        else:
            received(chunk, 3, 4, 5, 6)
            for turn in range(1, depth):
                line_sent(chunk, turn)
            for plan in range(7):
                each(chunk, lambda at, item: pair_copy(chunk, at, item, plan).wait_send())

    for chunk in range(len(chunks)):
        each(chunk, lambda at, item: own_copy(chunk, at, item).start())
    order = sorted(
        (number + 2 * chunk, chunk, number)
        for chunk in range(len(chunks))
        for number in range(depth + 4)
    )
    for _, chunk, number in order:
        stage(chunk, number)


def gather(arrays, chunks, collective_id):
    dp, shard = lax.axis_size("dp"), lax.axis_size("shard")
    narrow = min(array.shape[-2] for array in arrays)
    if (dp, shard) != (8, 4) or narrow % 8:
        return [
            lax.all_gather(array, AXES, axis=array.ndim - 2, tiled=True) for array in arrays
        ]
    depth = dp // 2
    shapes = [((1,) + array.shape)[-3:] for array in arrays]
    sizes = (len(chunks), max(len(chunk) for chunk in chunks))
    dma = pltpu.SemaphoreType.DMA
    results = pl.pallas_call(
        functools.partial(gather_kernel, len(arrays), shapes, chunks, depth),
        out_shape=[
            jax.ShapeDtypeStruct(
                ((lead,) if lead > 1 else ()) + (depth, 2, 2, 2, rows, cols), BF16
            )
            for lead, rows, cols in shapes
        ],
        in_specs=[whole(pl.ANY)] * len(arrays),
        out_specs=[whole(pl.ANY)] * len(arrays),
        scratch_shapes=[
            dma(sizes + (depth - 1, 2)),
            dma(sizes + (depth - 1, 2)),
            dma(sizes + (7,)),
            dma(sizes + (7,)),
            dma(sizes),
        ],
        compiler_params=pltpu.CompilerParams(
            collective_id=collective_id, has_side_effects=True, vmem_limit_bytes=1 << 20
        ),
        name="gather_weights",
    )(*arrays)
    return [
        result.reshape(((lead,) if lead > 1 else ()) + (dp * shard * rows, cols))
        for result, (lead, rows, cols) in zip(results, shapes)
    ]


def lane_index(rows):
    return lax.broadcasted_iota(jnp.int32, (rows, LANES), 1)


def halves(lane, odd):
    own = (lane >= HEAD_DIM) if odd else (lane < HEAD_DIM)
    other = lane if odd else lane - HEAD_DIM
    return own, other


def three_parts(values):
    high = values.astype(BF16).astype(F32)
    rest = values - high
    middle = rest.astype(BF16).astype(F32)
    return high, middle, rest - middle


def with_terms(own, other, values, terms):
    result = jnp.zeros_like(values)
    for at, term in enumerate(terms):
        result = jnp.where(other == at, term, result)
    return jnp.where(own, values, result)


def attend_kernel(student, lengths, *refs):
    if student:
        clip, x_ref, w_ref, b_ref, q_ref, k_ref, v_ref, ctx_ref, low_ref = refs

        @pl.when(pl.program_id(0) == 0)
        def _():
            width = saturation * clip[0]
            low_ref[...] = (width * jnp.tanh(x_ref[...].astype(F32) / width)).astype(BF16)

        inputs = low_ref[...]
    else:
        x_ref, w_ref, b_ref, q_ref, k_ref, ctx_ref = refs
        inputs = x_ref[...]
    rows = inputs.shape[0]
    lane = lane_index(rows)
    position = lax.broadcasted_iota(jnp.int32, (rows, LANES), 0)
    hidden_key = jnp.where(position < lengths[0], 0.0, masked_score)
    queries, keys, values = (
        (dot(inputs, w_ref[slot], 1, 1) + b_ref[slot]).astype(BF16) for slot in range(3)
    )
    if not student:
        q_ref[...] = queries
        k_ref[...] = keys
    block = 512
    for pair in range(2):
        lanes = slice(pair * LANES, (pair + 1) * LANES)
        query, key, value = (
            array[:, lanes].astype(F32) for array in (queries, keys, values)
        )
        parts = []
        for odd in range(2):
            own, other = halves(lane, odd)
            place = slice((pair * 2 + odd) * LANES, (pair * 2 + odd + 1) * LANES)
            query_full = with_terms(own, other, query, (0.0, 0.0, 0.0, 1.0)).astype(BF16)
            key_full = with_terms(own, other, key, (1.0, 1.0, 1.0, hidden_key)).astype(BF16)
            value_full = with_terms(own, other, value, (1.0, 1.0, 1.0)).astype(BF16)
            if student:
                k_ref[:, place] = key_full
                v_ref[:, place] = value_full
            found = []
            for start in range(0, rows, block):
                take = slice(start, start + block)
                scores = dot(query_full[take], key_full, 1, 1)
                top = jnp.max(scores, axis=1, keepdims=True)
                expo = jnp.exp2((scores - top) * exponent).astype(BF16)
                mixed = dot(expo, value_full, 1, 0)
                at = 0 if odd else HEAD_DIM
                total = mixed[:, at : at + 1]
                found.append(mixed / total)
                if student:
                    logsum = top + jnp.log(total) / scaling
                    q_ref[take, place] = with_terms(
                        own[take],
                        other[take],
                        query[take],
                        tuple(-part for part in three_parts(logsum)) + (1.0,),
                    ).astype(BF16)
            parts.append(jnp.concatenate(found, axis=0))
        context = jnp.where(lane < HEAD_DIM, parts[0], parts[1])
        ctx_ref[:, lanes] = context.astype(ctx_ref.dtype)


def attend(student, own_length, clip_scales, inputs, weights, bias):
    rows = inputs.shape[0]
    wide = 4 * LANES
    narrow = 2 * LANES
    scalar = whole(pltpu.SMEM)
    in_specs = [scalar] + ([scalar] if student else [])
    in_specs += [
        fixed((rows, D)),
        pl.BlockSpec((3, narrow, D), lambda i: (0, i, 0)),
        columns((3, 1, narrow)),
    ]
    if student:
        out_shape = [jax.ShapeDtypeStruct((rows, 2 * D), BF16)] * 3 + [
            jax.ShapeDtypeStruct((rows, D), F32),
            jax.ShapeDtypeStruct((rows, D), BF16),
        ]
        out_specs = [columns((rows, wide))] * 3 + [columns((rows, narrow)), fixed((rows, D))]
        args = (own_length, clip_scales, inputs, weights, bias)
    else:
        out_shape = [jax.ShapeDtypeStruct((rows, D), BF16)] * 3
        out_specs = [columns((rows, narrow))] * 3
        args = (own_length, inputs, weights, bias)
    return pl.pallas_call(
        functools.partial(attend_kernel, student),
        grid=(D // narrow,),
        in_specs=in_specs,
        out_specs=out_specs,
        out_shape=out_shape,
        compiler_params=pltpu.CompilerParams(vmem_limit_bytes=vmem_bytes),
        name="student_attention" if student else "teacher_attention",
    )(*args)


def split_dot(left, right):
    high = right.astype(BF16)
    low = (right - high.astype(F32)).astype(BF16)
    return dot(left, high, 1, 0) + dot(left, low, 1, 0)


def attend_back_kernel(
    lengths, inverse_pairs, q_ref, k_ref, v_ref, ctx_ref, dctx_ref, tq_ref, tk_ref, grad_ref, sum_ref
):
    rows = ctx_ref.shape[0]
    lane = lane_index(rows)
    position = lax.broadcasted_iota(jnp.int32, (rows, LANES), 0)
    live = position < lengths[0]
    low_half = lane < HEAD_DIM
    grad_context = dctx_ref[...].astype(F32)
    product = grad_context * ctx_ref[...]
    block = 512
    pieces = []
    for odd in range(2):
        own, other = halves(lane, odd)
        place = slice(odd * LANES, (odd + 1) * LANES)
        query, key, value = q_ref[:, place], k_ref[:, place], v_ref[:, place]
        weighted = jnp.sum(jnp.where(own, product, 0.0), axis=1, keepdims=True)
        grad_full = with_terms(
            own, other, grad_context, tuple(-part for part in three_parts(weighted))
        ).astype(BF16)
        grad_query = None
        key_parts, value_parts = [], []
        for start in range(0, rows, block):
            take = slice(start, start + block)
            probs = jnp.exp2(dot(key[take], query, 1, 1) * exponent)
            grad_scores = (probs * dot(value[take], grad_full, 1, 1)).astype(BF16)
            value_parts.append(dot(probs.astype(BF16), grad_full, 1, 0))
            key_parts.append(dot(grad_scores, query, 1, 0))
            part = dot(grad_scores, key[take], 0, 0)
            grad_query = part if grad_query is None else grad_query + part
        pieces.append(
            (grad_query, jnp.concatenate(key_parts, axis=0), jnp.concatenate(value_parts, axis=0))
        )
    query_live, key_live = (
        jnp.where(live, jnp.where(low_half, ref[:, :LANES], ref[:, LANES:]), 0.0).astype(BF16)
        for ref in (q_ref, k_ref)
    )
    teach_query, teach_key = (
        jnp.where(live, ref[...], 0.0).astype(BF16) for ref in (tq_ref, tk_ref)
    )
    row = lax.broadcasted_iota(jnp.int32, (LANES, LANES), 0)
    col = lax.broadcasted_iota(jnp.int32, (LANES, LANES), 1)
    same = (row < HEAD_DIM) == (col < HEAD_DIM)

    def gram(left, right):
        return jnp.where(same, outer_rows(left, right), 0.0)

    key_key, teach_key_key = gram(key_live, key_live), gram(teach_key, key_live)
    query_query, teach_query_query = gram(query_live, query_live), gram(teach_query, query_live)
    squares = (
        query_query * key_key
        - 2.0 * teach_query_query * teach_key_key
        + gram(teach_query, teach_query) * gram(teach_key, teach_key)
    )
    squares = jnp.sum(squares.reshape(LANES // 8, 8, LANES), axis=0)

    @pl.when(pl.program_id(0) == 0)
    def _():
        sum_ref[...] = jnp.zeros_like(sum_ref)

    sum_ref[...] += squares * (scaling * scaling * inverse_pairs[0])
    factor = 2.0 * scaling * scaling * inverse_pairs[0]
    query_term = split_dot(
        jnp.concatenate([query_live, teach_query], axis=1),
        jnp.concatenate([key_key, -teach_key_key], axis=0),
    )
    key_term = split_dot(
        jnp.concatenate([key_live, teach_key], axis=1),
        jnp.concatenate([query_query, -teach_query_query], axis=0),
    )
    (even_q, even_k, even_v), (odd_q, odd_k, odd_v) = pieces
    grad_ref[0] = (jnp.where(low_half, even_q, odd_q) * scaling + factor * query_term).astype(BF16)
    grad_ref[1] = (jnp.where(low_half, even_k, odd_k) * scaling + factor * key_term).astype(BF16)
    grad_ref[2] = jnp.where(low_half, even_v, odd_v).astype(BF16)


def attend_back(own_length, inverse_pairs, query, key, value, context, grad_context, tq, tk):
    rows = context.shape[0]
    scalar = whole(pltpu.SMEM)
    return pl.pallas_call(
        attend_back_kernel,
        grid=(D // LANES,),
        in_specs=[scalar, scalar]
        + [columns((rows, 2 * LANES))] * 3
        + [columns((rows, LANES))] * 4,
        out_specs=[columns((3, rows, LANES)), fixed((8, LANES))],
        out_shape=[
            jax.ShapeDtypeStruct((3, rows, D), BF16),
            jax.ShapeDtypeStruct((8, LANES), F32),
        ],
        compiler_params=pltpu.CompilerParams(vmem_limit_bytes=vmem_bytes),
        name="attention_backward",
    )(own_length, inverse_pairs, query, key, value, context, grad_context, tq, tk)


def gelu_parts(upper):
    cumulative = 0.5 * (1.0 + lax.erf(upper * (1.0 / math.sqrt(2.0))))
    return cumulative, upper * cumulative


ff_part = 1024


def teacher_kernel(tok_ref, ctx_ref, wo_ref, w1_ref, w2_ref, vec_ref, ub_ref, out_ref):
    vec = vec_ref[...]
    normed, _ = normalize(
        tok_ref[...].astype(F32) + dot(ctx_ref[...], wo_ref[...], 1, 1) + vec[3:4]
    )
    hidden = normed * vec[5:6] + vec[7:8]
    low = hidden.astype(BF16)
    lower = None
    for start in range(0, w1_ref.shape[0], ff_part):
        take = slice(start, start + ff_part)
        _, bent = gelu_parts(dot(low, w1_ref[take], 1, 1) + ub_ref[:, take])
        part = dot(bent.astype(BF16), w2_ref[:, take], 1, 1)
        lower = part if lower is None else lower + part
    final, _ = normalize(hidden + lower + vec[4:5])
    out_ref[...] = final * vec[6:7] + vec[8:9]


def teacher_tail(tokens, context, wo, w1, w2, vectors, up_bias):
    rows, wide = tokens.shape[0], w1.shape[0]
    block = 256
    return pl.pallas_call(
        teacher_kernel,
        grid=(rows // block,),
        in_specs=[
            row_blocks((block, D)),
            row_blocks((block, D)),
            fixed((D, D)),
            fixed((wide, D)),
            fixed((D, wide)),
            fixed(vectors.shape),
            fixed((1, wide)),
        ],
        out_specs=row_blocks((block, D)),
        out_shape=jax.ShapeDtypeStruct((rows, D), F32),
        compiler_params=pltpu.CompilerParams(vmem_limit_bytes=vmem_bytes),
        name="teacher_feed_forward",
    )(tokens, context, wo, w1, w2, vectors, up_bias)


def student_kernel(
    lengths,
    clip,
    tok_ref,
    cot_ref,
    teach_ref,
    ctx_ref,
    wo_ref,
    w1_ref,
    w2_ref,
    vec_ref,
    ub_ref,
    out_ref,
    dctx_ref,
    dao_ref,
    cb_ref,
    du_ref,
    hb_ref,
    df_ref,
    fb_ref,
    res_ref,
    sums_ref,
    upsum_ref,
    slope_ref,
):
    step = pl.program_id(0)
    vec = vec_ref[...]
    wide = w1_ref.shape[0]
    ctx_width, hid_width, act_width = (saturation * clip[at] for at in (1, 2, 3))
    ctx_bent = jnp.tanh(ctx_ref[...] / ctx_width)
    ctx_low = (ctx_width * ctx_bent).astype(BF16)
    cb_ref[...] = ctx_low
    first, first_inverse = normalize(
        tok_ref[...].astype(F32) + dot(ctx_low, wo_ref[...], 1, 1) + vec[3:4]
    )
    hidden = first * vec[5:6] + vec[7:8]
    hid_bent = jnp.tanh(hidden / hid_width)
    hid_low = (hid_width * hid_bent).astype(BF16)
    hb_ref[...] = hid_low
    lower = None
    for start in range(0, wide, ff_part):
        take = slice(start, start + ff_part)
        upper = dot(hid_low, w1_ref[take], 1, 1) + ub_ref[:, take]
        cumulative, bent = gelu_parts(upper)
        act = jnp.tanh(bent / act_width)
        density = jnp.exp(-0.5 * upper * upper) * (1.0 / math.sqrt(2.0 * math.pi))
        slope_ref[:, take] = (1.0 - act * act) * (cumulative + upper * density)
        act_low = (act_width * act).astype(BF16)
        fb_ref[:, take] = act_low
        part = dot(act_low, w2_ref[:, take], 1, 1)
        lower = part if lower is None else lower + part
    second, second_inverse = normalize(hidden + lower + vec[4:5])
    result = second * vec[6:7] + vec[8:9]
    out_ref[...] = result.astype(BF16)
    rows = result.shape[0]
    position = lax.broadcasted_iota(jnp.int32, (rows, D), 0) + step * rows
    gap = jnp.where(position < lengths[0], result - teach_ref[...], 0.0)
    grad_out = cot_ref[...].astype(F32) + gap * (2.0 * hidden_weight)
    grad_second = norm_back(grad_out * vec[6:7], second, second_inverse)
    grad_lower = grad_second.astype(BF16)
    df_ref[...] = grad_lower
    grad_hidden = None
    up_sums = []
    for start in range(0, wide, ff_part):
        take = slice(start, start + ff_part)
        grad_upper = (dot(grad_lower, w2_ref[:, take], 1, 0) * slope_ref[:, take]).astype(BF16)
        du_ref[:, take] = grad_upper
        up_sums.append(jnp.sum(grad_upper.astype(F32), axis=0, keepdims=True))
        part = dot(grad_upper, w1_ref[take], 1, 0)
        grad_hidden = part if grad_hidden is None else grad_hidden + part
    grad_hidden = grad_second + grad_hidden * (1.0 - hid_bent * hid_bent)
    grad_first = norm_back(grad_hidden * vec[5:6], first, first_inverse)
    res_ref[...] = grad_first
    grad_attn = grad_first.astype(BF16)
    dao_ref[...] = grad_attn
    dctx_ref[...] = (
        dot(grad_attn, wo_ref[...], 1, 0) * (1.0 - ctx_bent * ctx_bent)
    ).astype(BF16)

    @pl.when(step == 0)
    def _():
        sums_ref[...] = jnp.zeros_like(sums_ref)
        upsum_ref[...] = jnp.zeros_like(upsum_ref)

    for at, term in enumerate(
        (
            grad_attn.astype(F32),
            grad_lower.astype(F32),
            grad_hidden * first,
            grad_out * second,
            grad_hidden,
            grad_out,
            gap * gap,
        )
    ):
        sums_ref[at : at + 1] += jnp.sum(term, axis=0, keepdims=True)
    upsum_ref[...] += jnp.concatenate(up_sums, axis=1)


def student_middle(
    own_length, clip_scales, tokens, cotangent, teach_out, context, wo, w1, w2, vectors, up_bias
):
    rows, wide = tokens.shape[0], w1.shape[0]
    block = 256
    scalar = whole(pltpu.SMEM)
    narrow_spec, wide_spec = row_blocks((block, D)), row_blocks((block, wide))
    narrow, broad = jax.ShapeDtypeStruct((rows, D), BF16), jax.ShapeDtypeStruct((rows, wide), BF16)
    return pl.pallas_call(
        student_kernel,
        grid=(rows // block,),
        in_specs=[scalar, scalar]
        + [narrow_spec] * 4
        + [
            fixed((D, D)),
            fixed((wide, D)),
            fixed((D, wide)),
            fixed(vectors.shape),
            fixed((1, wide)),
        ],
        out_specs=[narrow_spec] * 4
        + [wide_spec, narrow_spec, narrow_spec, wide_spec, narrow_spec, fixed((8, D)), fixed((1, wide))],
        out_shape=[narrow] * 4
        + [
            broad,
            narrow,
            narrow,
            broad,
            jax.ShapeDtypeStruct((rows, D), F32),
            jax.ShapeDtypeStruct((8, D), F32),
            jax.ShapeDtypeStruct((1, wide), F32),
        ],
        scratch_shapes=[pltpu.VMEM((block, wide), F32)],
        compiler_params=pltpu.CompilerParams(vmem_limit_bytes=vmem_bytes),
        name="student_feed_forward",
    )(own_length, clip_scales, tokens, cotangent, teach_out, context, wo, w1, w2, vectors, up_bias)


def input_kernel(clip, grad_ref, w_ref, low_ref, tok_ref, res_ref, out_ref, dw_ref, sum_ref, acc_ref):
    slot = pl.program_id(0)
    grad = grad_ref[0]
    part = dot(grad, w_ref[0], 1, 0)
    dw_ref[0] = outer_rows(grad, low_ref[...]).astype(dw_ref.dtype)
    sum_ref[0] = jnp.sum(grad.astype(F32), axis=0, keepdims=True)

    @pl.when(slot == 0)
    def _():
        acc_ref[...] = part

    @pl.when(slot > 0)
    def _():
        acc_ref[...] += part

    @pl.when(slot == pl.num_programs(0) - 1)
    def _():
        bent = jnp.tanh(tok_ref[...].astype(F32) / (saturation * clip[0]))
        out_ref[...] = (res_ref[...] + acc_ref[...] * (1.0 - bent * bent)).astype(BF16)


def input_grads(clip_scales, grads, weights, low, tokens, residual):
    rows = tokens.shape[0]
    slotted = lambda *shape: pl.BlockSpec((1,) + shape, lambda i: (i, 0, 0))
    return pl.pallas_call(
        input_kernel,
        grid=(3,),
        in_specs=[
            whole(pltpu.SMEM),
            slotted(rows, D),
            slotted(D, D),
            fixed((rows, D)),
            fixed((rows, D)),
            fixed((rows, D)),
        ],
        out_specs=[fixed((rows, D)), slotted(D, D), slotted(1, D)],
        out_shape=[
            jax.ShapeDtypeStruct((rows, D), BF16),
            jax.ShapeDtypeStruct((3, D, D), F32),
            jax.ShapeDtypeStruct((3, 1, D), F32),
        ],
        scratch_shapes=[pltpu.VMEM((rows, D), F32)],
        compiler_params=pltpu.CompilerParams(vmem_limit_bytes=vmem_bytes),
        name="input_gradient",
    )(clip_scales, grads, weights, low, tokens, residual)


def on_device(
    tokens,
    teacher_tokens,
    cotangent,
    lengths,
    clip_scales,
    attn_latent,
    up_latent,
    down_latent,
    biases,
    up_bias,
    norm_gains,
    norm_shifts,
    teacher_attn,
    teacher_up,
    teacher_down,
    teacher_biases,
    teacher_up_bias,
    teacher_gains,
    teacher_shifts,
):
    count = lax.axis_size(AXES)
    narrow, wide = biases.shape[1], up_bias.shape[0]
    own_length = lax.dynamic_slice_in_dim(lengths, lax.axis_index(AXES), 1)
    live_float = lengths.astype(F32)
    token_norm = jnp.sum(live_float)
    pair_norm = HEADS * jnp.sum(live_float * live_float)
    inverse_pairs = (1.0 / pair_norm).reshape(1)
    vectors = jnp.concatenate(
        [teacher_biases, teacher_gains, teacher_shifts, biases, norm_gains, norm_shifts], axis=0
    )
    small = jnp.concatenate([vectors.reshape(-1), teacher_up_bias, up_bias])
    small = jnp.pad(small, (0, 8 * D - small.shape[0])).reshape(8, D)
    (
        small_all,
        teach_qkv,
        attn_w,
        teach_wo,
        teach_up,
        teach_down,
        up_w,
        down_w,
    ) = gather(
        [
            small,
            teacher_attn[:3],
            binarize(attn_latent),
            teacher_attn[3],
            teacher_up,
            teacher_down,
            binarize(up_latent),
            binarize(down_latent),
        ],
        ((0, 1), (2, 3), (4,), (5,), (6,), (7,)),
        0,
    )
    small_all = small_all.reshape(count, -1)
    lines = vectors.shape[0]
    vec = (
        small_all[:, : lines * narrow]
        .reshape(count, lines, narrow)
        .transpose(1, 0, 2)
        .reshape(lines, D)
        .astype(F32)
    )
    teach_vec, student_vec = vec[: lines // 2], vec[lines // 2 :]
    at = lines * narrow
    teach_up_bias = small_all[:, at : at + wide].reshape(1, -1).astype(F32)
    student_up_bias = small_all[:, at + wide : at + 2 * wide].reshape(1, -1).astype(F32)
    tq, tk, teach_context = attend(
        False, own_length, clip_scales, teacher_tokens, teach_qkv, teach_vec[:3].reshape(3, 1, D)
    )
    query, key, value, context, x_low = attend(
        True, own_length, clip_scales, tokens, attn_w[:3], student_vec[:3].reshape(3, 1, D)
    )
    teach_out = teacher_tail(
        teacher_tokens, teach_context, teach_wo, teach_up, teach_down, teach_vec, teach_up_bias
    )
    (
        result,
        grad_context,
        grad_attn,
        ctx_low,
        grad_upper,
        hid_low,
        grad_lower,
        act_low,
        residual,
        sums,
        up_sums,
    ) = student_middle(
        own_length,
        clip_scales,
        tokens,
        cotangent,
        teach_out,
        context,
        attn_w[3],
        up_w,
        down_w,
        student_vec,
        student_up_bias,
    )
    down_weight_grad = outer_rows(grad_lower, act_low)
    up_weight_grad = outer_rows(grad_upper, hid_low)
    out_weight_grad = outer_rows(grad_attn, ctx_low)
    grads, squares = attend_back(
        own_length, inverse_pairs, query, key, value, context, grad_context, tq, tk
    )
    input_grad, qkv_weight_grad, qkv_sums = input_grads(
        clip_scales, grads, attn_w[:3], x_low, tokens, residual
    )
    local_loss = jnp.sum(sums[6]) / (D * token_norm) + jnp.sum(squares)
    attn_weight_grad = jnp.concatenate([qkv_weight_grad, out_weight_grad[None]], axis=0)
    bias_terms = jnp.concatenate([qkv_sums[:, 0], sums[:2]], axis=0)
    lines = jnp.concatenate([bias_terms, sums[2:6]], axis=0)
    own_sums = jnp.concatenate(
        [
            lines.reshape(9, count, narrow).transpose(1, 0, 2).reshape(count, -1),
            up_sums.reshape(count, wide),
            jnp.broadcast_to(local_loss, (count, 1)),
        ],
        axis=1,
    )
    own_sums = jnp.pad(own_sums, ((0, 0), (0, D - own_sums.shape[1])))
    attn_total = lax.psum_scatter(attn_weight_grad, AXES, scatter_dimension=1, tiled=True)
    up_total = lax.psum_scatter(up_weight_grad, AXES, scatter_dimension=0, tiled=True)
    down_total = lax.psum_scatter(down_weight_grad, AXES, scatter_dimension=0, tiled=True)
    sum_total = lax.psum_scatter(own_sums, AXES, scatter_dimension=0, tiled=True)[0]
    line_total = sum_total[: 9 * narrow].reshape(9, narrow)
    up_bias_total = sum_total[9 * narrow : 9 * narrow + wide]
    loss = sum_total[9 * narrow + wide]
    return (
        result,
        loss,
        input_grad,
        latent_grad(attn_latent, attn_total),
        latent_grad(up_latent, up_total),
        latent_grad(down_latent, down_total),
        line_total[:5],
        up_bias_total,
        line_total[5:7],
        line_total[7:9],
    )
def solution(mesh):
    in_specs = (
        P(("dp", "shard"), None),
        P(("dp", "shard"), None),
        P(("dp", "shard"), None),
        P(),
        P(),
        P(None, ("dp", "shard"), None),
        P(("dp", "shard"), None),
        P(("dp", "shard"), None),
        P(None, ("dp", "shard")),
        P(("dp", "shard")),
        P(None, ("dp", "shard")),
        P(None, ("dp", "shard")),
        P(None, ("dp", "shard"), None),
        P(("dp", "shard"), None),
        P(("dp", "shard"), None),
        P(None, ("dp", "shard")),
        P(("dp", "shard")),
        P(None, ("dp", "shard")),
        P(None, ("dp", "shard")),
    )
    out_specs = (
        P(("dp", "shard"), None),
        P(),
        P(("dp", "shard"), None),
        P(None, ("dp", "shard"), None),
        P(("dp", "shard"), None),
        P(("dp", "shard"), None),
        P(None, ("dp", "shard")),
        P(("dp", "shard")),
        P(None, ("dp", "shard")),
        P(None, ("dp", "shard")),
    )
    return jax.shard_map(
        on_device, mesh=mesh, in_specs=in_specs, out_specs=out_specs, check_vma=False
    )
```

time: 1100 us -> 941 us (0.86)
  matrix products: 491 us -> 23.7 us
  waiting for transfers between devices: 76.7 us -> 508 us
  Pallas kernels: 0 us -> 313 us
  blocking collectives: 309 us -> 0 us
  other arithmetic: 84.5 us -> 27.6 us
  local copies, waits for them, and re-layouts: 100 us -> 43.3 us
  loops' own time: 12.2 us -> 0 us
    dot_general x34 -> x3, matrix products: 384 us -> 23.7 us  [dot(): lax.dot_general(left, right, (((left_dim,), (right_dim,)), ((), ())), pre...]
    reduce_scatter x3, waiting for transfers between devices: 74.4 us -> 414 us  [the longest x1 140 us: on_device(): lax.psum_scatter(attn_weight_grad, AXES, scatter_dimension=1, tiled=True)]
    pallas_call x0 -> x7, Pallas kernels: none -> 313 us  [the longest x1 138 us: gather(): pl.pallas_call(functools.partial(gather_kernel, len(arrays), shapes, chun...]
    all_gather x6 -> x0, blocking collectives: 233 us -> none  [the longest x1 44 us: on_device(): lax.all_gather(teacher_biases, ('dp', 'shard'), axis=1, tiled=True)]
    sub x4 -> x0, matrix products: 107 us -> none  [the longest x2 80.3 us: attend_one_block(): grad_probs - weighted]
    unnamed x9 -> x5, waiting for transfers between devices: 2.16 us -> 93.1 us
    psum x1 -> x0, blocking collectives: 38.1 us -> none  [on_device(): loss = lax.psum(local_loss, ('dp', 'shard'))]
    unnamed x1 -> x0, blocking collectives: 37.8 us -> none
  transfers between devices with their start and end apart: 9 -> 4, of which waited for: 1 -> 4; matrix products, arithmetic and copies ran while one was open for 58% -> 4% of each run, Pallas kernels for 0% -> 0%
where the time goes in v2:
time: 941 us; the launch traced here: 933 us
  waiting for transfers between devices  508 us (54%)
  Pallas kernels  313 us (33%)
  local copies, waits for them, and re-layouts  43.3 us (5%)
  other arithmetic  27.6 us (3%)
  matrix products  23.7 us (3%)
  between operations  17.2 us (2%)
    reduce_scatter x1, waiting for transfers between devices, on_device(): lax.psum_scatter(attn_weight_grad, AXES, scatter_dimension=1, tiled=True)  140 us
    reduce_scatter x1, waiting for transfers between devices, on_device(): lax.psum_scatter(up_weight_grad, AXES, scatter_dimension=0, tiled=True)  140 us
    pallas_call x1, Pallas kernels, gather(): pl.pallas_call(functools.partial(gather_kernel, len(arrays), shapes, chun...  138 us
    reduce_scatter x1, waiting for transfers between devices, on_device(): lax.psum_scatter(down_weight_grad, AXES, scatter_dimension=0, tiled=True)  135 us
    unnamed x5, waiting for transfers between devices  93.1 us
    pallas_call x2, Pallas kernels, attend(): pl.pallas_call(functools.partial(attend_kernel, student), grid=(D // narr...  51.7 us
    pallas_call x1, Pallas kernels, attend_back(): pl.pallas_call(attend_back_kernel, grid=(D // LANES,), in_specs=[scalar,...  45.2 us
    pallas_call x1, Pallas kernels, student_middle(): pl.pallas_call(student_kernel, grid=(rows // block,), in_specs=[scalar, s...  42 us
  transfers between devices with their start and end apart: 4, of which 4 were waited for; matrix products, arithmetic and copies ran while one was open for 4% of the time, Pallas kernels for 0%

profile of v2, /device:TPU:0, one launch (start us, length us, event | category | flops | bytes accessed | tf_op | source)
XLA Modules:
  0.0 932.6 jit_solution(1402627488006688691)
XLA Ops:
  15.3 2.8 concatenate.21
  20.9 138.2 %gather_weights.1 = (bf16[4,2,2,2,8,768]{5,4,3,2,1,0:T(8,128)(2,1)S(1)}, bf16[3,4,2,2,2,24,768]{6,5,4,3,2,1,0:T(8,128)(2,1)S(1)}, bf16[4,4,2,2,2,24,768]{6,5,4,3...) custom-call(bf16[8,768]{1,0:T(8,128)(2,1)S(1)} %reshape.142.refs_0_,, ...), custom_call_target="tpu_custom_call" | custom-call | tf_op jit(solution)/shard_map/gather_weights/pallas_call | solution.py:249
  159.1 2.2 copy-done
  161.4 2.1 copy-done.1
  163.5 2.2 copy-done.2
  165.7 2.1 copy-done.3
  167.8 2.2 copy-done.4
  170.0 1.8 copy-done.5
  173.1 4.1 slice.96
  177.2 2.4 slice.99
  185.5 23.8 %teacher_attention.1 = (bf16[1024,768]{1,0:T(8,128)(2,1)}, bf16[1024,768]{1,0:T(8,128)(2,1)}, bf16[1024,768]{1,0:T(8,128)(2,1)}) custom-call(s32[1]{0:T(128)} %dynamic_slice.3.lengths, bf16[1024,768]{1,0:T(8,128)(2,1)} %tok_ref.3, bf16[3,768,768]{2,1,0:T(8,128)(2,1)} %bitcast.38, f32[3,1,768]{2,1,0:T(1,128)} %reshape.157.refs_2_), custom_call_target="tpu_custom_call" | custom-call | tf_op jit(solution)/shard_map/teacher_attention/pallas_call | solution.py:385
  209.2 27.9 %student_attention.1 = (bf16[1024,1536]{1,0:T(8,128)(2,1)}, bf16[1024,1536]{1,0:T(8,128)(2,1)}, bf16[1024,1536]{1,0:T(8,128)(2,1)}, f32[1024,768]{1,0:T(8,128)}, bf16[1024,768]{1,0:T(8,128)(2,1)}) custom-call(s32[1]{0:T(128)} %dynamic_slice.3.lengths, f32[4]{0:T(128)} %clip.3, bf16[1024,768]{1,0:T(8,128)(2,1)} %tok_ref.5, bf16[3,768,768]{2,1,0:T(8,128)(2,1)} %bitcast.41, ...), custom_call_target="tpu_custom_call" | custom-call | tf_op jit(solution)/shard_map/student_attention/pallas_call | solution.py:385
  237.2 20.9 %teacher_feed_forward.1.teach_ref = f32[1024,768]{1,0:T(8,128)} custom-call(bf16[1024,768]{1,0:T(8,128)(2,1)} %tok_ref.3, bf16[1024,768]{1,0:T(8,128)(2,1)} %get-tuple-element.44.ctx_ref, bf16[768,768]{1,0:T(8,128)(2,1)} %bitcast.39, bf16[3072,768]{1,0:T(8,128)(2,1)} %bitcast.34, bf16[768,3072]{1,0:T(8,128)(2,1)} %bitcast.35, f32[9,768]{1,0:T(8,128)} %slice.94.vec_ref, ...), custom_call_target="tpu_custom_call" | custom-call | tf_op jit(solution)/shard_map/teacher_feed_forward/pallas_call | solution.py:525
  258.1 42.0 %student_feed_forward.1 = (bf16[1024,768]{1,0:T(8,128)(2,1)}, bf16[1024,768]{1,0:T(8,128)(2,1)}, bf16[1024,768]{1,0:T(8,128)(2,1)}, bf16[1024,768]{1,0:T(8,128)(...) custom-call(s32[1]{0:T(128)} %dynamic_slice.3.lengths, ...), custom_call_target="tpu_custom_call" | custom-call | tf_op jit(solution)/shard_map/student_feed_forward/pallas_call | solution.py:651
  300.1 1.4 slice_reduce_fusion
  302.1 45.2 %attention_backward.1 = (bf16[3,1024,768]{2,1,0:T(8,128)(2,1)}, f32[8,128]{1,0:T(8,128)}) custom-call(s32[1]{0:T(128)} %dynamic_slice.3.lengths, f32[1]{0:T(128)} %bitcast.12.inverse_pairs, bf16[1024,1536]{1,0:T(8,128)(2,1)} %get-tuple-element.53.q_ref, bf16[1024,1536]{1,0:T(8,128)(2,1)} %get-tuple-element.54.k_ref, ...), custom_call_target="tpu_custom_call" | custom-call | tf_op jit(solution)/shard_map/attention_backward/pallas_call | solution.py:481
  347.4 15.2 %input_gradient.1 = (bf16[1024,768]{1,0:T(8,128)(2,1)}, f32[3,768,768]{2,1,0:T(8,128)}, f32[3,1,768]{2,1,0:T(1,128)}) custom-call(f32[4]{0:T(128)} %clip.3, bf16[3,1024,768]{2,1,0:T(8,128)(2,1)} %get-tuple-element.59.grad_ref, bf16[3,768,768]{2,1,0:T(8,128)(2,1)} %bitcast.42, bf16[1024,768]{1,0:T(8,128)(2,1)} %get-tuple-element.60.low_ref, ...), custom_call_target="tpu_custom_call" | custom-call | tf_op jit(solution)/shard_map/input_gradient/pallas_call | solution.py:705
  368.6 10.6 %fusion.8 = f32[768,3072]{1,0:T(8,128)} fusion(bf16[1024,768]{1,0:T(8,128)(2,1)S(1)} %copy-done.17, bf16[1024,3072]{1,0:T(8,128)(2,1)} %get-tuple-element.73), kind=kOutput, calls=%fused_computation.42 | convolution fusion | flops 4831838208 | bytes 17301504 | tf_op jit(solution)/shard_map/dot_general | solution.py:32
  379.2 1.3 copy-done.16
  380.6 10.2 %fusion.7 = f32[3072,768]{1,0:T(8,128)} fusion(bf16[1024,3072]{1,0:T(8,128)(2,1)} %get-tuple-element.70, bf16[1024,768]{1,0:T(8,128)(2,1)S(1)} %copy-done.16), kind=kOutput, calls=%fused_computation.41 | convolution fusion | flops 4831838208 | bytes 17301504 | tf_op jit(solution)/shard_map/dot_general | solution.py:32
  390.8 1.3 copy-done.15
  392.2 2.9 convolution_bitcast_fusion
  395.1 7.5 pad_maximum_fusion
  402.6 93.1 %all-reduce.5.cloned.1.call-done = f32[32,768]{0,1:T(8,128)} async-done(((f32[32,768]{0,1:T(8,128)}), f32[32,768]{0,1:T(8,128)}) %all-reduce.5.cloned.1.call-update) | async-done | bytes 98320
  499.7 1.3 dynamic-slice.1
  500.9 1.5 dynamic-slice_reduce_fusion.1
  502.4 134.6 %reduce-scatter.9.cloned.1.call-done = f32[24,3072]{1,0:T(8,128)} async-done(((f32[768,3072]{1,0:T(8,128)}), f32[24,3072]{1,0:T(8,128)}) %reduce-scatter.9.cloned.1.call-update) | async-done | bytes 294928 | tf_op jit(solution)/shard_map/reduce_scatter | solution.py:855
  638.2 139.6 %reduce-scatter.7.cloned.1.call-done = f32[96,768]{1,0:T(8,128)} async-done(((f32[3072,768]{1,0:T(8,128)}), f32[96,768]{1,0:T(8,128)}) %reduce-scatter.7.cloned.1.call-update) | async-done | bytes 294928 | tf_op jit(solution)/shard_map/reduce_scatter | solution.py:854
  778.8 140.3 %reduce-scatter.5.cloned.1.call-done = f32[4,24,768]{2,1,0:T(8,128)} async-done(((f32[4,768,768]{2,1,0:T(8,128)}), f32[4,24,768]{2,1,0:T(8,128)}) %reduce-scatter.5.cloned.1.call-update) | async-done | bytes 294928 | tf_op jit(solution)/shard_map/reduce_scatter | solution.py:853
  920.2 1.8 negate_add_fusion
  922.0 1.8 negate_add_fusion.1
  923.8 1.8 negate_add_fusion.2
  (95 shorter events, 29.4 us)
Async XLA Ops:
  7.2 488.5 %all-reduce.5.cloned.1.call-start = ((), (), s32[]{:S(2)}) async-start(), calls=%async_computation.6 | async-start | bytes 786432
  19.1 0.9 copy-start.7
  20.0 0.9 copy-start.8
  159.1 2.2 copy-start
  161.4 2.1 copy-start.1
  163.5 2.2 copy-start.2
  165.7 2.1 copy-start.3
  167.8 2.2 copy-start.4
  170.0 1.8 copy-start.5
  171.8 1.0 copy-start.6
  173.1 6.5 copy-start.18
  347.3 16.0 %copy-start.12 = (f32[8,768]{1,0:T(8,128)S(1)}, f32[8,768]{1,0:T(8,128)}, u32[]{:S(2)}) copy-start(f32[8,768]{1,0:T(8,128)} %get-tuple-element.63) | copy-start | bytes 73732
  347.3 16.8 %copy-start.13 = (f32[1,3072]{1,0:T(1,128)S(1)}, f32[1,3072]{1,0:T(1,128)}, u32[]{:S(2)}) copy-start(f32[1,3072]{1,0:T(1,128)} %get-tuple-element.64) | copy-start | bytes 36868
  347.3 17.6 %copy-start.14 = (f32[8,128]{1,0:T(8,128)S(1)}, f32[8,128]{1,0:T(8,128)}, u32[]{:S(2)}) copy-start(f32[8,128]{1,0:T(8,128)} %get-tuple-element.65) | copy-start | bytes 12292
  347.3 21.2 %copy-start.17 = (bf16[1024,768]{1,0:T(8,128)(2,1)S(1)}, bf16[1024,768]{1,0:T(8,128)(2,1)}, u32[]{:S(2)}) copy-start(bf16[1024,768]{1,0:T(8,128)(2,1)} %get-tuple-element.72) | copy-start | bytes 4718596
  368.5 268.5 %reduce-scatter.9.cloned.1.call-start = ((), (), s32[]{:S(2)}) async-start(), calls=%async_computation.5 | async-start | bytes 9732096 | tf_op jit(solution)/shard_map/reduce_scatter | solution.py:855
  379.1 1.4 copy-start.16
  379.2 398.6 %reduce-scatter.7.cloned.1.call-start = ((), (), s32[]{:S(2)}) async-start(), calls=%async_computation.4 | async-start | bytes 9732096 | tf_op jit(solution)/shard_map/reduce_scatter | solution.py:854
  390.8 1.4 copy-start.15
  390.8 528.3 %reduce-scatter.5.cloned.1.call-start = ((), (), s32[]{:S(2)}) async-start(), calls=%async_computation.3 | async-start | bytes 9732096 | tf_op jit(solution)/shard_map/reduce_scatter | solution.py:853
  402.6 234.5 %copy-start.10 = (f32[24,3072]{1,0:T(8,128)S(1)}, f32[24,3072]{1,0:T(8,128)}, u32[]{:S(2)}) copy-start(f32[24,3072]{1,0:T(8,128)} %param.26) | copy-start | bytes 884740
  402.6 375.2 %copy-start.11 = (f32[96,768]{1,0:T(8,128)S(1)}, f32[96,768]{1,0:T(8,128)}, u32[]{:S(2)}) copy-start(f32[96,768]{1,0:T(8,128)} %param.25) | copy-start | bytes 884740
  402.6 516.6 %copy-start.9 = (f32[4,24,768]{2,1,0:T(8,128)S(1)}, f32[4,24,768]{2,1,0:T(8,128)}, u32[]{:S(2)}) copy-start(f32[4,24,768]{2,1,0:T(8,128)} %param.24) | copy-start | bytes 884740
Sparse Core Ops, SparseCore 0:
  368.6 126.9 all-reduce.4
  502.6 134.4 reduce-scatter.8
  643.0 134.7 reduce-scatter.6
  784.5 134.5 reduce-scatter.4

commit v3 on v2

--- a/solution.py
+++ b/solution.py
@@ -82,53 +82,96 @@
     return pl.BlockSpec(shape, lambda i: (i,) + (0,) * (len(shape) - 1))
 
 
-def gather_kernel(count, shapes, chunks, depth, *refs):
-    ins, outs = refs[:count], refs[count : 2 * count]
-    line_send, line_recv, pair_send, pair_recv, own_sem = refs[2 * count :]
-    dp, shard = lax.axis_index("dp"), lax.axis_index("shard")
-    z, y = dp // 2, lax.rem(dp, 2)
-    x, core = shard // 2, lax.rem(shard, 2)
-
-    def device(z_at, y_at, x_at, core_at):
-        return (z_at * 2 + y_at, x_at * 2 + core_at)
-
-    above = device(jnp.minimum(z + 1, depth - 1), y, x, core)
-    below = device(jnp.maximum(z - 1, 0), y, x, core)
-    y_one, x_one = lax.rem(y + 1 - core, 2), lax.rem(x + core, 2)
-    y_two, x_two = lax.rem(y + core, 2), lax.rem(x + 1 - core, 2)
-    first, second = device(z, y_one, x_one, core), device(z, y_two, x_two, core)
-    sibling = device(z, y, x, 1 - core)
-    barrier = pltpu.get_barrier_semaphore()
-    for partner in (first, second, sibling):
-        pl.semaphore_signal(barrier, inc=1, device_id=partner, device_id_type=MESH)
-
-    @pl.when(z < depth - 1)
-    def _():
-        pl.semaphore_signal(barrier, inc=1, device_id=above, device_id_type=MESH)
-
-    @pl.when(z > 0)
-    def _():
-        pl.semaphore_signal(barrier, inc=1, device_id=below, device_id_type=MESH)
-
-    pl.semaphore_wait(barrier, 3 + jnp.minimum(z, 1) + jnp.minimum(depth - 1 - z, 1))
+class Place:
+    def __init__(self, depth):
+        self.depth = depth
+        dp, shard = lax.axis_index("dp"), lax.axis_index("shard")
+        z, y = dp // 2, lax.rem(dp, 2)
+        x, core = shard // 2, lax.rem(shard, 2)
+        self.z, self.y, self.x, self.core = z, y, x, core
+
+        def device(z_at, y_at, x_at, core_at):
+            return (z_at * 2 + y_at, x_at * 2 + core_at)
+
+        self.above = device(jnp.minimum(z + 1, depth - 1), y, x, core)
+        self.below = device(jnp.maximum(z - 1, 0), y, x, core)
+        one = (lax.rem(y + 1 - core, 2), lax.rem(x + core, 2))
+        two = (lax.rem(y + core, 2), lax.rem(x + 1 - core, 2))
+        self.pieces = ((y, x), one, two, (1 - y, 1 - x))
+        self.first, self.second = device(z, *one, core), device(z, *two, core)
+        self.sibling = device(z, y, x, 1 - core)
+
+    def barrier(self):
+        semaphore = pltpu.get_barrier_semaphore()
+        for partner in (self.first, self.second, self.sibling):
+            pl.semaphore_signal(semaphore, inc=1, device_id=partner, device_id_type=MESH)
+
+        @pl.when(self.z < self.depth - 1)
+        def _():
+            pl.semaphore_signal(semaphore, inc=1, device_id=self.above, device_id_type=MESH)
+
+        @pl.when(self.z > 0)
+        def _():
+            pl.semaphore_signal(semaphore, inc=1, device_id=self.below, device_id_type=MESH)
+
+        pl.semaphore_wait(
+            semaphore, 3 + jnp.minimum(self.z, 1) + jnp.minimum(self.depth - 1 - self.z, 1)
+        )
+
+
+def remote(source, target, send_sem, recv_sem, device):
+    return pltpu.make_async_remote_copy(
+        src_ref=source,
+        dst_ref=target,
+        send_sem=send_sem,
+        recv_sem=recv_sem,
+        device_id=device,
+        device_id_type=MESH,
+    )
+
+
+def tiled_over(mesh_sizes, rows):
+    return mesh_sizes == (8, 4) and rows % 8 == 0
+
+
+def in_order(counts, apart):
+    return [
+        (chunk, number)
+        for _, chunk, number in sorted(
+            (number + apart * chunk, chunk, number)
+            for chunk, count in enumerate(counts)
+            for number in range(count)
+        )
+    ]
+
+
+def gather_scratch(chunks, depth):
+    dma = pltpu.SemaphoreType.DMA
+    sizes = (len(chunks), max(len(chunk) for chunk in chunks))
+    return [
+        dma(sizes + (depth - 1, 2)),
+        dma(sizes + (depth - 1, 2)),
+        dma(sizes + (7,)),
+        dma(sizes + (7,)),
+        dma(sizes),
+    ]
+
+
+def gather_stages(place, ins, outs, leads, chunks, sems, apart=2):
+    line_send, line_recv, pair_send, pair_recv, own_sem = sems
+    depth, z, y, x, core = place.depth, place.z, place.y, place.x, place.core
 
     def slot(item, *index):
-        return outs[item].at[((slice(None),) if shapes[item][0] > 1 else ()) + index]
+        return outs[item].at[((slice(None),) if leads[item] > 1 else ()) + index]
 
     def line_copy(chunk, at, item, turn, upward):
         if upward:
-            owner, target = jnp.maximum(z - (turn - 1), 0), above
+            owner, target = jnp.maximum(z - (turn - 1), 0), place.above
         else:
-            owner, target = jnp.minimum(z + (turn - 1), depth - 1), below
+            owner, target = jnp.minimum(z + (turn - 1), depth - 1), place.below
         block = slot(item, owner, y, x, core)
-        return pltpu.make_async_remote_copy(
-            src_ref=block,
-            dst_ref=block,
-            send_sem=line_send.at[chunk, at, turn - 1, int(upward)],
-            recv_sem=line_recv.at[chunk, at, turn - 1, int(upward)],
-            device_id=target,
-            device_id_type=MESH,
-        )
+        where = (chunk, at, turn - 1, int(upward))
+        return remote(block, block, line_send.at[where], line_recv.at[where], target)
 
     def sends(turn, upward):
         if upward:
@@ -144,26 +187,20 @@
         )
 
     plans = (
-        ((y, x), first),
-        ((y, x), second),
-        ((y_one, x_one), second),
-        ((y, x), sibling),
-        ((y_one, x_one), sibling),
-        ((y_two, x_two), sibling),
-        ((1 - y, 1 - x), sibling),
+        (0, place.first),
+        (0, place.second),
+        (1, place.second),
+        (0, place.sibling),
+        (1, place.sibling),
+        (2, place.sibling),
+        (3, place.sibling),
     )
 
     def pair_copy(chunk, at, item, plan):
-        (y_at, x_at), target = plans[plan]
-        block = slot(item, slice(None), y_at, x_at, core)
-        return pltpu.make_async_remote_copy(
-            src_ref=block,
-            dst_ref=block,
-            send_sem=pair_send.at[chunk, at, plan],
-            recv_sem=pair_recv.at[chunk, at, plan],
-            device_id=target,
-            device_id_type=MESH,
-        )
+        piece, target = plans[plan]
+        block = slot(item, slice(None), *place.pieces[piece], core)
+        where = (chunk, at, plan)
+        return remote(block, block, pair_send.at[where], pair_recv.at[where], target)
 
     def each(chunk, action):
         for at, item in enumerate(chunks[chunk]):
@@ -224,53 +261,289 @@
             for plan in range(7):
                 each(chunk, lambda at, item: pair_copy(chunk, at, item, plan).wait_send())
 
-    for chunk in range(len(chunks)):
-        each(chunk, lambda at, item: own_copy(chunk, at, item).start())
-    order = sorted(
-        (number + 2 * chunk, chunk, number)
-        for chunk in range(len(chunks))
-        for number in range(depth + 4)
-    )
-    for _, chunk, number in order:
-        stage(chunk, number)
+    def begin():
+        for chunk in range(len(chunks)):
+            each(chunk, lambda at, item: own_copy(chunk, at, item).start())
+
+    return [begin] + [
+        functools.partial(stage, chunk, number)
+        for chunk, number in in_order([depth + 4] * len(chunks), apart)
+    ]
+
+
+def gather_shapes(arrays, depth):
+    shapes = [((1,) + array.shape)[-3:] for array in arrays]
+    leads = [shape[0] for shape in shapes]
+    results = [
+        jax.ShapeDtypeStruct(((lead,) if lead > 1 else ()) + (depth, 2, 2, 2, rows, cols), BF16)
+        for lead, rows, cols in shapes
+    ]
+    return leads, results
+
+
+def gathered(results):
+    return [
+        result.reshape(result.shape[:-6] + (-1, result.shape[-1])) for result in results
+    ]
+
+
+def gather_kernel(leads, chunks, depth, *refs):
+    count = len(leads)
+    place = Place(depth)
+    place.barrier()
+    for stage in gather_stages(
+        place, refs[:count], refs[count : 2 * count], leads, chunks, refs[2 * count :]
+    ):
+        stage()
 
 
 def gather(arrays, chunks, collective_id):
     dp, shard = lax.axis_size("dp"), lax.axis_size("shard")
-    narrow = min(array.shape[-2] for array in arrays)
-    if (dp, shard) != (8, 4) or narrow % 8:
+    if not tiled_over((dp, shard), min(array.shape[-2] for array in arrays)):
         return [
             lax.all_gather(array, AXES, axis=array.ndim - 2, tiled=True) for array in arrays
         ]
     depth = dp // 2
-    shapes = [((1,) + array.shape)[-3:] for array in arrays]
-    sizes = (len(chunks), max(len(chunk) for chunk in chunks))
-    dma = pltpu.SemaphoreType.DMA
+    leads, results = gather_shapes(arrays, depth)
     results = pl.pallas_call(
-        functools.partial(gather_kernel, len(arrays), shapes, chunks, depth),
-        out_shape=[
-            jax.ShapeDtypeStruct(
-                ((lead,) if lead > 1 else ()) + (depth, 2, 2, 2, rows, cols), BF16
-            )
-            for lead, rows, cols in shapes
-        ],
+        functools.partial(gather_kernel, leads, chunks, depth),
+        out_shape=results,
         in_specs=[whole(pl.ANY)] * len(arrays),
         out_specs=[whole(pl.ANY)] * len(arrays),
-        scratch_shapes=[
-            dma(sizes + (depth - 1, 2)),
-            dma(sizes + (depth - 1, 2)),
-            dma(sizes + (7,)),
-            dma(sizes + (7,)),
-            dma(sizes),
-        ],
+        scratch_shapes=gather_scratch(chunks, depth),
         compiler_params=pltpu.CompilerParams(
             collective_id=collective_id, has_side_effects=True, vmem_limit_bytes=1 << 20
         ),
         name="gather_weights",
     )(*arrays)
+    return gathered(results)
+
+
+def scatter_scratch(shapes, dtypes, depth):
+    dma = pltpu.SemaphoreType.DMA
+    scratch = []
+    for shape, dtype in zip(shapes, dtypes):
+        lead, rows, cols = shape
+        block = (depth, lead, rows, cols)
+        scratch += [
+            pltpu.VMEM((4,) + block, dtype),
+            pltpu.VMEM((4,) + block, dtype),
+            pltpu.VMEM((3,) + block, dtype),
+            pltpu.VMEM((2,) + block, dtype),
+        ]
+    count = len(shapes)
+    return scratch + [
+        dma((count, 4)),
+        dma((count, 7)),
+        dma((count, 7)),
+        dma((count, depth, 2)),
+        dma((count, depth, 2)),
+    ]
+
+
+def scatter_stages(place, ins, outs, scratch, count, apart=2):
+    depth, z, core = place.depth, place.z, place.core
+    own_sem, pair_send, pair_recv, line_send, line_recv = scratch[4 * count :]
+
+    def buffers(item):
+        return scratch[4 * item : 4 * item + 4]
+
+    def source(item, piece, lead, side):
+        index = (slice(None),) + place.pieces[piece] + (side,)
+        ref = ins[item]
+        return ref.at[((lead,) if ref.shape[:-6] else ()) + index]
+
+    def leads(item):
+        return range(buffers(item)[0].shape[2])
+
+    def own_copy(item, piece, lead):
+        held = buffers(item)[0]
+        return pltpu.make_async_copy(
+            source(item, piece, lead, core), held.at[piece, :, lead], own_sem.at[item, piece]
+        )
+
+    names = (0, 2, 1, 3)
+
+    def core_copy(item, piece, lead):
+        arrived = buffers(item)[1]
+        name = names[piece]
+        return remote(
+            source(item, piece, lead, 1 - core),
+            arrived.at[name, :, lead],
+            pair_send.at[item, piece],
+            pair_recv.at[item, name],
+            place.sibling,
+        )
+
+    def core_wait(item, piece):
+        arrived = buffers(item)[1]
+        block = arrived.at[piece]
+        remote(
+            block, block, pair_send.at[item, piece], pair_recv.at[item, piece], place.sibling
+        ).wait_recv()
+
+    def chip_copy(item, plan):
+        held, _, arrived, _ = buffers(item)
+        piece, target = ((2, place.second), (3, place.second), (1, place.first))[plan]
+        return remote(
+            held.at[piece],
+            arrived.at[plan],
+            pair_send.at[item, 4 + plan],
+            pair_recv.at[item, 4 + plan],
+            target,
+        )
+
+    def line_copy(item, owner, upward, fresh):
+        held, _, _, arrived = buffers(item)
+        block = arrived.at[int(upward), owner]
+        where = (item, owner, int(upward))
+        return remote(
+            held.at[0, owner] if fresh else block,
+            block,
+            line_send.at[where],
+            line_recv.at[where],
+            place.above if upward else place.below,
+        )
+
+    def add(target, *others):
+        def one(at):
+            total = target[at].astype(F32)
+            for other in others:
+                total = total + other[at].astype(F32)
+            target[at] = total.astype(target.dtype)
+
+        for first in range(target.shape[0]):
+            for second in range(target.shape[1]):
+                one((first, second))
+
+    def add_block(target, other):
+        for lead in range(target.shape[0]):
+            target[lead] = (target[lead].astype(F32) + other[lead].astype(F32)).astype(
+                target.dtype
+            )
+
+    def merge(item, piece):
+        held, arrived, _, _ = buffers(item)
+        block = held.at[piece]
+        pltpu.make_async_copy(block, block, own_sem.at[item, piece]).wait()
+        core_wait(item, piece)
+        add(block, arrived.at[piece])
+
+    def line_turn(item, turn, upward):
+        held, _, _, arrived = buffers(item)
+        at = turn if upward else depth - 1 - turn
+        beyond = range(at + 1, depth) if upward else range(at)
+
+        @pl.when(z == at)
+        def _():
+            for owner in sorted(beyond, key=lambda owner: -abs(owner - at)):
+                if turn:
+                    line_copy(item, owner, upward, False).wait_recv()
+                    add_block(arrived.at[int(upward), owner], held.at[0, owner])
+                line_copy(item, owner, upward, not turn).start()
+            if turn:
+                line_copy(item, at, upward, False).wait_recv()
+
+    def stage(item, number):
+        held, _, arrived, line = buffers(item)
+        if number == 0:
+            for piece in (3, 1, 2, 0):
+                for lead in leads(item):
+                    core_copy(item, piece, lead).start()
+            for piece in (2, 3, 1, 0):
+                for lead in leads(item):
+                    own_copy(item, piece, lead).start()
+        elif number == 1:
+            for piece, plan in ((3, 1), (2, 0)):
+                merge(item, piece)
+                chip_copy(item, plan).start()
+        elif number == 2:
+            merge(item, 1)
+            merge(item, 0)
+        elif number == 3:
+            chip_copy(item, 1).wait_recv()
+            add(held.at[1], arrived.at[1])
+            chip_copy(item, 2).start()
+        elif number == 4:
+            chip_copy(item, 0).wait_recv()
+            chip_copy(item, 2).wait_recv()
+            add(held.at[0], arrived.at[0], arrived.at[2])
+            for upward in (True, False):
+                line_turn(item, 0, upward)
+        elif number < 4 + depth:
+            for upward in (True, False):
+                line_turn(item, number - 4, upward)
+        else:
+            for lead in leads(item):
+                outs[item][lead] = held[0, z, lead].astype(F32)
+
+            for upward, other in ((1, z > 0), (0, z < depth - 1)):
+
+                @pl.when(other)
+                def _():
+                    for lead in leads(item):
+                        outs[item][lead] += line[upward, z, lead].astype(F32)
+
+            for piece in range(4):
+                block = buffers(item)[1].at[piece]
+                remote(
+                    block, block, pair_send.at[item, piece], pair_recv.at[item, piece], place.sibling
+                ).wait_send()
+            for plan in range(3):
+                chip_copy(item, plan).wait_send()
+            for upward in (True, False):
+                for owner in range(depth):
+
+                    @pl.when((z < owner) if upward else (z > owner))
+                    def _():
+                        line_copy(item, owner, upward, False).wait_send()
+
     return [
-        result.reshape(((lead,) if lead > 1 else ()) + (dp * shard * rows, cols))
-        for result, (lead, rows, cols) in zip(results, shapes)
+        functools.partial(stage, item, number)
+        for item, number in in_order([5 + depth] * count, apart)
+    ]
+
+
+def scatter_kernel(count, depth, *refs):
+    place = Place(depth)
+    place.barrier()
+    for stage in scatter_stages(
+        place, refs[:count], refs[count : 2 * count], refs[2 * count :], count
+    ):
+        stage()
+
+
+def split_rows(array, depth):
+    return array.reshape(array.shape[:-2] + (depth, 2, 2, 2, -1, array.shape[-1]))
+
+
+def scatter(arrays, collective_id):
+    dp, shard = lax.axis_size("dp"), lax.axis_size("shard")
+    owned = min(array.shape[-2] for array in arrays) // (dp * shard)
+    if not tiled_over((dp, shard), owned):
+        return [
+            lax.psum_scatter(
+                array.astype(F32), AXES, scatter_dimension=array.ndim - 2, tiled=True
+            )
+            for array in arrays
+        ]
+    depth = dp // 2
+    arrays = [split_rows(array, depth) for array in arrays]
+    shapes = [(math.prod(array.shape[:-6]),) + array.shape[-2:] for array in arrays]
+    results = pl.pallas_call(
+        functools.partial(scatter_kernel, len(arrays), depth),
+        out_shape=[jax.ShapeDtypeStruct(shape, F32) for shape in shapes],
+        in_specs=[whole(pl.ANY)] * len(arrays),
+        out_specs=[whole()] * len(arrays),
+        scratch_shapes=scatter_scratch(shapes, [array.dtype for array in arrays], depth),
+        compiler_params=pltpu.CompilerParams(
+            collective_id=collective_id, has_side_effects=True, vmem_limit_bytes=vmem_bytes
+        ),
+        name="scatter_gradients",
+    )(*arrays)
+    return [
+        result.reshape(array.shape[:-6] + result.shape[1:])
+        for result, array in zip(results, arrays)
     ]
 
 
@@ -716,7 +989,7 @@
         out_specs=[fixed((rows, D)), slotted(D, D), slotted(1, D)],
         out_shape=[
             jax.ShapeDtypeStruct((rows, D), BF16),
-            jax.ShapeDtypeStruct((3, D, D), F32),
+            jax.ShapeDtypeStruct((3, D, D), BF16),
             jax.ShapeDtypeStruct((3, 1, D), F32),
         ],
         scratch_shapes=[pltpu.VMEM((rows, D), F32)],
@@ -838,7 +1111,6 @@
         clip_scales, grads, attn_w[:3], x_low, tokens, residual
     )
     local_loss = jnp.sum(sums[6]) / (D * token_norm) + jnp.sum(squares)
-    attn_weight_grad = jnp.concatenate([qkv_weight_grad, out_weight_grad[None]], axis=0)
     bias_terms = jnp.concatenate([qkv_sums[:, 0], sums[:2]], axis=0)
     lines = jnp.concatenate([bias_terms, sums[2:6]], axis=0)
     own_sums = jnp.concatenate(
@@ -849,11 +1121,19 @@
         ],
         axis=1,
     )
-    own_sums = jnp.pad(own_sums, ((0, 0), (0, D - own_sums.shape[1])))
-    attn_total = lax.psum_scatter(attn_weight_grad, AXES, scatter_dimension=1, tiled=True)
-    up_total = lax.psum_scatter(up_weight_grad, AXES, scatter_dimension=0, tiled=True)
-    down_total = lax.psum_scatter(down_weight_grad, AXES, scatter_dimension=0, tiled=True)
-    sum_total = lax.psum_scatter(own_sums, AXES, scatter_dimension=0, tiled=True)[0]
+    own_sums = jnp.pad(own_sums, ((0, 0), (0, 8 * LANES - own_sums.shape[1])))
+    down_total, up_total, out_total, qkv_total, sum_total = scatter(
+        [
+            down_weight_grad.astype(BF16),
+            up_weight_grad.astype(BF16),
+            out_weight_grad.astype(BF16),
+            qkv_weight_grad,
+            own_sums.reshape(count * 8, LANES),
+        ],
+        1,
+    )
+    attn_total = jnp.concatenate([qkv_total, out_total[None]], axis=0)
+    sum_total = sum_total.reshape(-1)
     line_total = sum_total[: 9 * narrow].reshape(9, narrow)
     up_bias_total = sum_total[9 * narrow : 9 * narrow + wide]
     loss = sum_total[9 * narrow + wide]

time: 941 us -> 486 us (0.52)
  waiting for transfers between devices: 508 us -> 0 us
  Pallas kernels: 313 us -> 403 us
  between operations: 17.2 us -> 4.21 us
  other arithmetic: 27.6 us -> 17.5 us
  local copies, waits for them, and re-layouts: 43.3 us -> 33.3 us
    reduce_scatter x3 -> x0, waiting for transfers between devices: 414 us -> none  [the longest x1 140 us: on_device(): lax.psum_scatter(attn_weight_grad, AXES, scatter_dimension=1, tiled=True)]
    unnamed x5 -> x0, waiting for transfers between devices: 93.1 us -> none
    pallas_call x1 -> x2, Pallas kernels: 138 us -> 229 us  [the longest x1 138 us: gather(): pl.pallas_call(functools.partial(gather_kernel, leads, chunks, depth), ou...]
  transfers between devices with their start and end apart: 4 -> 0, of which waited for: 4 -> 0; matrix products, arithmetic and copies ran while one was open for 4% -> 0% of each run, Pallas kernels for 0% -> 0%
where the time goes in v3:
time: 486 us; the launch traced here: 477 us
  Pallas kernels  403 us (83%)
  local copies, waits for them, and re-layouts  33.3 us (7%)
  matrix products  18.3 us (4%)
  other arithmetic  17.5 us (4%)
    pallas_call x1, Pallas kernels, gather(): pl.pallas_call(functools.partial(gather_kernel, leads, chunks, depth), ou...  138 us
    pallas_call x1, Pallas kernels, scatter(): pl.pallas_call(functools.partial(scatter_kernel, len(arrays), depth), out...  90.4 us
    pallas_call x2, Pallas kernels, attend(): pl.pallas_call(functools.partial(attend_kernel, student), grid=(D // narr...  51.2 us
    pallas_call x1, Pallas kernels, attend_back(): pl.pallas_call(attend_back_kernel, grid=(D // LANES,), in_specs=[scalar,...  45.2 us
    pallas_call x1, Pallas kernels, student_middle(): pl.pallas_call(student_kernel, grid=(rows // block,), in_specs=[scalar, s...  42 us
    pallas_call x1, Pallas kernels, teacher_tail(): pl.pallas_call(teacher_kernel, grid=(rows // block,), in_specs=[row_block...  21.4 us
    dot_general x3, matrix products, dot(): lax.dot_general(left, right, (((left_dim,), (right_dim,)), ((), ())), pre...  18.3 us
    pallas_call x1, Pallas kernels, input_grads(): pl.pallas_call(input_kernel, grid=(3,), in_specs=[whole(pltpu.SMEM), slot...  15.1 us

profile of v3, /device:TPU:0, one launch (start us, length us, event | category | flops | bytes accessed | tf_op | source)
XLA Modules:
  0.0 476.7 jit_solution(6603595831477408076)
XLA Ops:
  0.8 1.3 dynamic_slice.3.lengths
  2.1 1.1 abs_reduce_fusion.2
  3.2 1.1 multiply_convert_fusion.2.refs_2_
  4.2 1.1 abs_reduce_fusion
  5.3 1.1 multiply_convert_fusion.refs_7_
  6.4 1.1 abs_reduce_fusion.1
  7.5 1.1 multiply_convert_fusion.1.refs_6_
  10.7 138.3 %gather_weights.1 = (bf16[4,2,2,2,8,768]{5,4,3,2,1,0:T(8,128)(2,1)S(1)}, bf16[3,4,2,2,2,24,768]{6,5,4,3,2,1,0:T(8,128)(2,1)S(1)}, bf16[4,4,2,2,2,24,768]{6,5,4,3...) custom-call(bf16[8,768]{1,0:T(8,128)(2,1)S(1)} %reshape.161.refs_0_,, ...), custom_call_target="tpu_custom_call" | custom-call | tf_op jit(solution)/shard_map/gather_weights/pallas_call | solution.py:308
  149.0 2.2 copy-done
  151.2 2.2 copy-done.1
  153.3 2.1 copy-done.2
  155.5 2.1 copy-done.3
  157.5 2.1 copy-done.4
  159.7 1.9 copy-done.5
  161.5 1.0 copy-done.6
  163.6 23.8 %teacher_attention.1 = (bf16[1024,768]{1,0:T(8,128)(2,1)}, bf16[1024,768]{1,0:T(8,128)(2,1)}, bf16[1024,768]{1,0:T(8,128)(2,1)}) custom-call(s32[1]{0:T(128)} %dynamic_slice.3.lengths, bf16[1024,768]{1,0:T(8,128)(2,1)} %tok_ref.3, bf16[3,768,768]{2,1,0:T(8,128)(2,1)} %bitcast.61, f32[3,1,768]{2,1,0:T(1,128)} %reshape.182.refs_2_), custom_call_target="tpu_custom_call" | custom-call | tf_op jit(solution)/shard_map/teacher_attention/pallas_call | solution.py:658
  189.0 21.4 %teacher_feed_forward.1.teach_ref = f32[1024,768]{1,0:T(8,128)} custom-call(bf16[1024,768]{1,0:T(8,128)(2,1)} %tok_ref.3, bf16[1024,768]{1,0:T(8,128)(2,1)} %get-tuple-element.49.ctx_ref, bf16[768,768]{1,0:T(8,128)(2,1)} %bitcast.62, bf16[3072,768]{1,0:T(8,128)(2,1)} %bitcast.57, bf16[768,3072]{1,0:T(8,128)(2,1)} %bitcast.58, f32[9,768]{1,0:T(8,128)} %slice.95.vec_ref, ...), custom_call_target="tpu_custom_call" | custom-call | tf_op jit(solution)/shard_map/teacher_feed_forward/pallas_call | solution.py:798
  211.2 4.1 slice.97
  215.3 27.4 %student_attention.1 = (bf16[1024,1536]{1,0:T(8,128)(2,1)}, bf16[1024,1536]{1,0:T(8,128)(2,1)}, bf16[1024,1536]{1,0:T(8,128)(2,1)}, f32[1024,768]{1,0:T(8,128)}, bf16[1024,768]{1,0:T(8,128)(2,1)}) custom-call(s32[1]{0:T(128)} %dynamic_slice.3.lengths, f32[4]{0:T(128)} %clip.3, bf16[1024,768]{1,0:T(8,128)(2,1)} %tok_ref.5, bf16[3,768,768]{2,1,0:T(8,128)(2,1)} %bitcast.64, ...), custom_call_target="tpu_custom_call" | custom-call | tf_op jit(solution)/shard_map/student_attention/pallas_call | solution.py:658
  244.2 2.4 slice.100
  246.6 42.0 %student_feed_forward.1 = (bf16[1024,768]{1,0:T(8,128)(2,1)}, bf16[1024,768]{1,0:T(8,128)(2,1)}, bf16[1024,768]{1,0:T(8,128)(2,1)}, bf16[1024,768]{1,0:T(8,128)(...) custom-call(s32[1]{0:T(128)} %dynamic_slice.3.lengths, ...), custom_call_target="tpu_custom_call" | custom-call | tf_op jit(solution)/shard_map/student_feed_forward/pallas_call | solution.py:924
  289.9 45.2 %attention_backward.1 = (bf16[3,1024,768]{2,1,0:T(8,128)(2,1)}, f32[8,128]{1,0:T(8,128)}) custom-call(s32[1]{0:T(128)} %dynamic_slice.3.lengths, f32[1]{0:T(128)} %bitcast.15.inverse_pairs, bf16[1024,1536]{1,0:T(8,128)(2,1)} %get-tuple-element.64.q_ref, bf16[1024,1536]{1,0:T(8,128)(2,1)} %get-tuple-element.65.k_ref, ...), custom_call_target="tpu_custom_call" | custom-call | tf_op jit(solution)/shard_map/attention_backward/pallas_call | solution.py:754
  335.1 1.3 reduce_sum.98
  339.0 15.1 %input_gradient.1 = (bf16[1024,768]{1,0:T(8,128)(2,1)}, bf16[3,768,768]{2,1,0:T(8,128)(2,1)}, f32[3,1,768]{2,1,0:T(1,128)}) custom-call(f32[4]{0:T(128)} %clip.3, bf16[3,1024,768]{2,1,0:T(8,128)(2,1)} %get-tuple-element.70.grad_ref, bf16[3,768,768]{2,1,0:T(8,128)(2,1)} %bitcast.65, bf16[1024,768]{1,0:T(8,128)(2,1)} %get-tuple-element.71.low_ref, ...), custom_call_target="tpu_custom_call" | custom-call | tf_op jit(solution)/shard_map/input_gradient/pallas_call | solution.py:978
  357.3 4.3 convolution_convert_fusion.2
  361.6 7.1 %convolution_convert_fusion = bf16[3072,768]{1,0:T(8,128)(2,1)} fusion(bf16[1024,3072]{1,0:T(8,128)(2,1)S(1)} %copy-done.25, bf16[1024,768]{1,0:T(8,128)(2,1)S(1)} %copy-done.27), kind=kOutput, calls=%fused_computation | convolution fusion | flops 4834197504 | bytes 12582912 | tf_op jit(solution)/shard_map/dot_general | solution.py:32
  368.7 7.0 %convolution_convert_fusion.1 = bf16[768,3072]{1,0:T(8,128)(2,1)} fusion(bf16[1024,768]{1,0:T(8,128)(2,1)S(1)} %copy-done.26, bf16[1024,3072]{1,0:T(8,128)(2,1)S(1)} %bitcast.82), kind=kOutput, calls=%fused_computation.1 | convolution fusion | flops 4834197504 | bytes 12582912 | tf_op jit(solution)/shard_map/dot_general | solution.py:32
  375.7 90.4 %scatter_gradients.1 = (f32[1,24,3072]{2,1,0:T(8,128)}, f32[1,96,768]{2,1,0:T(8,128)}, f32[1,24,768]{2,1,0:T(8,128)}, f32[3,24,768]{2,1,0:T(8,128)}, f32[1,8,128]{2,1,0:T(8,128)}) custom-call(bf16[4,2,2,2,24,3072]{5,4,3,2,1,0:T(8,128)(2,1)} %bitcast.68, bf16[4,2,2,2,96,768]{5,4,3,2,1,0:T(8,128)(2,1)} %bitcast.67, bf16[4,2,2,2,24,768]{5,4,3,2,1,0:T(8,128)(2,1)} %bitcast.70, ...), custom_call_target="tpu_custom_call" | custom-call | tf_op jit(solution)/shard_map/scatter_gradients/pallas_call | solution.py:533
  466.1 1.2 fusion.2
  467.3 1.8 fusion.1
  469.1 1.1 fusion.5
  470.2 1.8 fusion.4
  (113 shorter events, 15.8 us)
Async XLA Ops:
  0.6 9.6 %copy-start.17 = (bf16[5,24]{1,0:T(8,128)(2,1)S(1)}, bf16[5,24]{1,0:T(8,128)(2,1)}, u32[]{:S(2)}) copy-start(bf16[5,24]{1,0:T(8,128)(2,1)} %param.27) | copy-start | bytes 724
  0.7 9.6 %copy-start.20 = (bf16[2,24]{1,0:T(2,128)(2,1)S(1)}, bf16[2,24]{1,0:T(2,128)(2,1)}, u32[]{:S(2)}) copy-start(bf16[2,24]{1,0:T(2,128)(2,1)} %param.29) | copy-start | bytes 292
  0.7 9.5 %copy-start.21 = (bf16[2,24]{1,0:T(2,128)(2,1)S(1)}, bf16[2,24]{1,0:T(2,128)(2,1)}, u32[]{:S(2)}) copy-start(bf16[2,24]{1,0:T(2,128)(2,1)} %param.30) | copy-start | bytes 292
  0.7 9.5 %copy-start.16 = (bf16[5,24]{1,0:T(8,128)(2,1)S(1)}, bf16[5,24]{1,0:T(8,128)(2,1)}, u32[]{:S(2)}) copy-start(bf16[5,24]{1,0:T(8,128)(2,1)} %param.34) | copy-start | bytes 724
  0.7 9.5 %copy-start.18 = (bf16[2,24]{1,0:T(2,128)(2,1)S(1)}, bf16[2,24]{1,0:T(2,128)(2,1)}, u32[]{:S(2)}) copy-start(bf16[2,24]{1,0:T(2,128)(2,1)} %param.36) | copy-start | bytes 292
  0.7 9.5 %copy-start.19 = (bf16[2,24]{1,0:T(2,128)(2,1)S(1)}, bf16[2,24]{1,0:T(2,128)(2,1)}, u32[]{:S(2)}) copy-start(bf16[2,24]{1,0:T(2,128)(2,1)} %param.37) | copy-start | bytes 292
  0.7 9.8 %copy-start.22 = (bf16[96]{0:T(256)(128)(2,1)S(1)}, bf16[96]{0:T(256)(128)(2,1)}, u32[]{:S(2)}) copy-start(bf16[96]{0:T(256)(128)(2,1)} %param.28) | copy-start | bytes 580
  0.7 9.8 %copy-start.23 = (bf16[96]{0:T(256)(128)(2,1)S(1)}, bf16[96]{0:T(256)(128)(2,1)}, u32[]{:S(2)}) copy-start(bf16[96]{0:T(256)(128)(2,1)} %param.35) | copy-start | bytes 580
  0.7 9.9 %copy-start.7 = (bf16[96,768]{1,0:T(8,128)(2,1)S(1)}, bf16[96,768]{1,0:T(8,128)(2,1)}, u32[]{:S(2)}) copy-start(bf16[96,768]{1,0:T(8,128)(2,1)} %refs_4_.1) | copy-start | bytes 442372
  0.7 9.9 %copy-start.8 = (bf16[24,3072]{1,0:T(8,128)(2,1)S(1)}, bf16[24,3072]{1,0:T(8,128)(2,1)}, u32[]{:S(2)}) copy-start(bf16[24,3072]{1,0:T(8,128)(2,1)} %refs_5_.1) | copy-start | bytes 442372
  149.0 2.2 copy-start
  151.1 2.2 copy-start.1
  153.3 2.1 copy-start.2
  155.5 2.1 copy-start.3
  157.5 2.1 copy-start.4
  159.7 1.9 copy-start.5
  161.5 1.0 copy-start.6
  246.6 42.0 %copy-start.29 = (s32[32]{0:T(128)S(1)}, s32[32]{0:T(128)}, u32[]{:S(2)}) copy-start(s32[32]{0:T(128)} %param.22) | copy-start | bytes 388
  289.9 46.5 %copy-start.14 = (f32[8,768]{1,0:T(8,128)S(1)}, f32[8,768]{1,0:T(8,128)}, u32[]{:S(2)}) copy-start(f32[8,768]{1,0:T(8,128)} %get-tuple-element.75) | copy-start | bytes 73732
  339.0 16.7 %copy-start.15 = (f32[1,3072]{1,0:T(1,128)S(1)}, f32[1,3072]{1,0:T(1,128)}, u32[]{:S(2)}) copy-start(f32[1,3072]{1,0:T(1,128)} %get-tuple-element.76) | copy-start | bytes 36868
  339.0 18.3 %copy-start.28 = (bf16[1024,768]{1,0:T(8,128)(2,1)S(1)}, bf16[1024,768]{1,0:T(8,128)(2,1)}, u32[]{:S(2)}) copy-start(bf16[1024,768]{1,0:T(8,128)(2,1)} %get-tuple-element.62) | copy-start | bytes 4718596
  356.6 5.0 %copy-start.25 = (bf16[1024,3072]{1,0:T(8,128)(2,1)S(1)}, bf16[1024,3072]{1,0:T(8,128)(2,1)}, u32[]{:S(2)}) copy-start(bf16[1024,3072]{1,0:T(8,128)(2,1)} %get-tuple-element.60) | copy-start | bytes 18874372
  356.6 5.0 %copy-start.27 = (bf16[1024,768]{1,0:T(8,128)(2,1)S(1)}, bf16[1024,768]{1,0:T(8,128)(2,1)}, u32[]{:S(2)}) copy-start(bf16[1024,768]{1,0:T(8,128)(2,1)} %get-tuple-element.61) | copy-start | bytes 4718596
  357.3 11.4 %slice-start = ((s8[6291456]{0:T(1024)(128)(4,1)}), s8[4194304]{0:T(1024)(128)(4,1)S(1)}, s32[]{:S(2)}) async-start(s8[6291456]{0:T(1024)(128)(4,1)} %bitcast.81), calls=%async_computation | async-start | bytes 8388608
  361.6 7.1 %slice-start.1 = ((s8[6291456]{0:T(1024)(128)(4,1)}), s8[2097152]{0:T(1024)(128)(4,1)S(1)}, s32[]{:S(2)}) async-start(s8[6291456]{0:T(1024)(128)(4,1)} %bitcast.81), calls=%async_computation.1 | async-start | bytes 4194304
  361.6 7.1 %copy-start.26 = (bf16[1024,768]{1,0:T(8,128)(2,1)S(1)}, bf16[1024,768]{1,0:T(8,128)(2,1)}, u32[]{:S(2)}) copy-start(bf16[1024,768]{1,0:T(8,128)(2,1)} %get-tuple-element.58) | copy-start | bytes 4718596
  375.7 90.4 %copy-start.10 = (f32[24,3072]{1,0:T(8,128)S(1)}, f32[24,3072]{1,0:T(8,128)}, u32[]{:S(2)}) copy-start(f32[24,3072]{1,0:T(8,128)} %param.26) | copy-start | bytes 884740
  375.7 93.4 %copy-start.11 = (f32[96,768]{1,0:T(8,128)S(1)}, f32[96,768]{1,0:T(8,128)}, u32[]{:S(2)}) copy-start(f32[96,768]{1,0:T(8,128)} %param.25) | copy-start | bytes 884740
  466.1 6.0 %copy-start.12 = (f32[3,24,768]{2,1,0:T(8,128)S(1)}, f32[3,24,768]{2,1,0:T(8,128)}, u32[]{:S(2)}) copy-start(f32[3,24,768]{2,1,0:T(8,128)} %get-tuple-element.80) | copy-start | bytes 663556
  466.1 6.0 %copy-start.13 = (f32[1,24,768]{2,1,0:T(8,128)S(1)}, f32[1,24,768]{2,1,0:T(8,128)}, u32[]{:S(2)}) copy-start(f32[1,24,768]{2,1,0:T(8,128)} %get-tuple-element.81) | copy-start | bytes 221188
  466.1 6.0 %copy-start.9 = (f32[4,24,768]{2,1,0:T(8,128)S(1)}, f32[4,24,768]{2,1,0:T(8,128)}, u32[]{:S(2)}) copy-start(f32[4,24,768]{2,1,0:T(8,128)} %param.24) | copy-start | bytes 884740
  467.3 5.8 %copy-start.24 = (f32[1,8,128]{2,1,0:T(8,128)S(1)}, f32[1,8,128]{2,1,0:T(8,128)}, u32[]{:S(2)}) copy-start(f32[1,8,128]{2,1,0:T(8,128)} %get-tuple-element.78) | copy-start | bytes 12292
